TPU v7x, 512 devices: a whole 4x8x8 slice. The times are simulated.
512 devices in a mesh: section: 2 (over core), region: 256 (over z, y, x).
Axes of the slice: x: 4, y: 8, z: 8, core: 2. Of those that a mesh axis runs over, the one named last changes fastest.
Arguments:
- hits: bfloat16 [2, 65536, 512], P('section', 'region'), may hold values from -6 to 6
- order: int32 [2, 256, 256], P(None, 'region'), may hold values from 0 to 255, each once within a row
- links: int32 [2, 512, 3], P(None, 'region'), may hold values from 0 to 511, as said below
- counts: int32 [2, 256], replicated, may hold values from 64 to 256, as said below
- w_qkv: bfloat16 [2, 512, 1536], P('section')
- w_out: bfloat16 [2, 512, 512], P('section'), may hold values from -0.25 to 0.25
- w_up: bfloat16 [2, 512, 2048], P('section'), may hold values from -0.25 to 0.25
- w_down: bfloat16 [2, 2048, 512], P('section'), may hold values from -0.125 to 0.125
Outputs:
- encoded: bfloat16 [2, 65536, 512], P('section', 'region')
Inputs may be any that keep to these rules, and one draw needn't show every extreme that they name: `links`: entry 0 of patch g is g itself; the other entries are distinct patches other than g, at most 2 patches away from g along the curve. `counts`: in every event some region is full and some region holds 64 hits. `order`: each region's entries along the last dimension list each of its 256 hits once.
All inputs are finite; a program needn't handle non-finite values.
Results may differ from a plain program's by a relative error of at most 0.015.
Values may be sent and summed in bfloat16 or wider, within the bound.
No kernel may reach another device: no remote copies, remote signals or barrier semaphores. Data moves between devices by JAX's collectives and lax.ppermute only.
A program may use at most 64 MiB of HBM per device.

v0:
```python
import jax
import jax.numpy as jnp
from jax import lax
from jax.sharding import PartitionSpec as P

HEADS = 8
REACH = 2


epsilon = 1e-05


def with_halo(cells, sides, width):
    for axis, dim in sides:
        count = lax.axis_size(axis)
        ends = count - 1
        head = lax.slice_in_dim(cells, 0, width, axis=dim)
        tail = lax.slice_in_dim(cells, cells.shape[dim] - width, cells.shape[dim], axis=dim)
        cells = jnp.concatenate(
            [
                lax.ppermute(tail, axis, [(i, (i + 1) % count) for i in range(ends)]),
                cells,
                lax.ppermute(head, axis, [((i + 1) % count, i) for i in range(ends)]),
            ],
            axis=dim,
        )
    return cells


def passed_along(value, axis, by):
    size = lax.axis_size(axis)
    pairs = [(i, i + by) for i in range(size) if 0 <= i + by < size]
    return lax.ppermute(value, axis, pairs)


def normalize(state):
    values = state.astype(jnp.float32)
    center = jnp.mean(values, axis=-1, keepdims=True)
    spread = jnp.mean((values - center) ** 2, axis=-1, keepdims=True)
    return ((values - center) * lax.rsqrt(spread + epsilon)).astype(jnp.bfloat16)


def attend(queries, near_keys, near_values, key_valid, local_links, patch_rows):
    patch_count = local_links.shape[0]
    links_count = local_links.shape[1]
    feature_width = queries.shape[1]
    head_width = feature_width // HEADS
    query_part = queries.reshape(patch_count, patch_rows, HEADS, head_width)
    key_part = near_keys.reshape(-1, patch_rows, HEADS, head_width)[local_links]
    key_part = key_part.reshape(patch_count, links_count * patch_rows, HEADS, head_width)
    value_part = near_values.reshape(-1, patch_rows, HEADS, head_width)[local_links]
    value_part = value_part.reshape(patch_count, links_count * patch_rows, HEADS, head_width)
    key_mask = key_valid.reshape(-1, patch_rows)[local_links].reshape(
        patch_count, links_count * patch_rows
    )
    scores = jnp.einsum(
        "pqhd,pkhd->phqk", query_part, key_part, preferred_element_type=jnp.float32
    ) * head_width ** (-0.5)
    scores = jnp.where(key_mask[:, None, None, :], scores, -1e30)
    highest = jnp.max(scores, axis=-1, keepdims=True)
    weights = jnp.exp(scores - highest)
    probs = (weights / jnp.sum(weights, axis=-1, keepdims=True)).astype(jnp.bfloat16)
    output = jnp.einsum("phqk,pkhd->pqhd", probs, value_part, preferred_element_type=jnp.float32)
    return output.reshape(patch_count * patch_rows, feature_width).astype(jnp.bfloat16)


def per_device(hits, order, links, counts, w_qkv, w_out, w_up, w_down):
    segments = lax.axis_size("section")
    segment_index = lax.axis_index("section")
    region_index = lax.axis_index("region")
    row_count = hits.shape[1]
    feature_width = hits.shape[2]
    patch_count = links.shape[1]
    patch_rows = row_count // patch_count
    margin = REACH * patch_rows
    region_total = counts.shape[1]
    slot_ids = jnp.arange(row_count + 2 * margin)
    place = region_index * row_count - margin + slot_ids
    owner = place // row_count
    inside = (place >= 0) & (place < region_total * row_count)
    offset = place - owner * row_count
    region_ids = jnp.arange(region_total)

    def run_block(state, event_index):
        count_row = counts[event_index]
        key_count = jnp.sum(
            jnp.where(owner[:, None] == region_ids[None, :], count_row[None, :], 0), axis=1
        )
        key_valid = inside & (offset < key_count)
        local_links = links[event_index] - region_index * patch_count + REACH
        weight_qkv = w_qkv[0]
        normed = normalize(state)
        mixed = jnp.dot(normed, weight_qkv, preferred_element_type=jnp.float32).astype(jnp.bfloat16)
        queries = mixed[:, :feature_width]
        paired = jnp.stack(
            [mixed[:, feature_width : 2 * feature_width], mixed[:, 2 * feature_width :]]
        )
        widened = with_halo(paired, (("region", 1),), margin)
        near_keys = widened[0]
        near_values = widened[1]
        attended = attend(queries, near_keys, near_values, key_valid, local_links, patch_rows)
        middle = (
            state.astype(jnp.float32)
            + jnp.dot(attended, w_out[0], preferred_element_type=jnp.float32)
        ).astype(jnp.bfloat16)
        normed_mlp = normalize(middle)
        hidden = jax.nn.gelu(
            jnp.dot(normed_mlp, w_up[0], preferred_element_type=jnp.float32), approximate=False
        ).astype(jnp.bfloat16)
        state = (
            middle.astype(jnp.float32)
            + jnp.dot(hidden, w_down[0], preferred_element_type=jnp.float32)
        ).astype(jnp.bfloat16)
        return state

    every_event = lax.all_gather(hits, "section", axis=0, tiled=True)
    collected = jnp.zeros((segments, row_count, feature_width), jnp.bfloat16)

    def step_once(tick_index, carry):
        state, gathered_out = carry
        event_index = jnp.clip(tick_index - segment_index, 0, segments - 1)
        fresh = lax.dynamic_index_in_dim(
            every_event, jnp.minimum(tick_index, segments - 1), 0, keepdims=False
        )
        arranged = fresh[order[event_index, 0]]
        current = jnp.where(segment_index == 0, arranged, state)
        result = run_block(current, event_index)
        passed = passed_along(result, "section", 1)
        gathered_out = lax.dynamic_update_index_in_dim(gathered_out, result, event_index, 0)
        return (passed, gathered_out)

    start_state = jnp.zeros((row_count, feature_width), jnp.bfloat16)
    final_carry = lax.fori_loop(0, 2 * segments - 1, step_once, (start_state, collected))
    finished = final_carry[1]
    spread_out = lax.all_to_all(finished, "section", split_axis=0, concat_axis=0, tiled=True)
    final_rows = spread_out[segments - 1]
    own_count = counts[segment_index, region_index]
    keep_rows = jnp.arange(row_count) < own_count
    return jnp.where(keep_rows[:, None], final_rows, jnp.zeros_like(final_rows))[None]


def solution(mesh):
    in_specs = (
        P("section", "region", None),
        P(None, "region", None),
        P(None, "region", None),
        P(),
        P("section", None, None),
        P("section", None, None),
        P("section", None, None),
        P("section", None, None),
    )
    out_specs = P("section", "region", None)
    return jax.shard_map(
        per_device, mesh=mesh, in_specs=in_specs, out_specs=out_specs, check_vma=False
    )
```

profile of v0, /device:TPU:255, one launch (start us, length us, event | category | flops | bytes accessed | tf_op | source)
XLA Modules:
  0.0 162.8 jit_solution(12706287801728999917)
XLA Ops:
  0.0 2.7 %all_gather.3 = bf16[2,256,512]{2,1,0:T(8,128)(2,1)S(1)} all-gather(bf16[1,256,512]{2,1,0:T(8,128)(2,1)} %param.10), channel_id=1, replica_groups=mesh['section'=2,'region'=256] {'section'}, dimensions={0}, use_global_device_ids=true | all-gather | bytes 786432 | tf_op jit(solution)/shard_map/all_gather | solution.py:116
  3.5 152.9 %while.19 = (s32[]{:T(128)}, bf16[256,512]{1,0:T(8,128)(2,1)S(1)}, bf16[2,256,512]{2,1,0:T(8,128)(2,1)}, pred[]{:T(512)}, bf16[2,256,512]{2,1,0:T(8,128)(2,1)S(1...) while((s32[]{:T(128)}, bf16[256,512]{1,0:T(8,128)(2,1)S(1)}, ...), condition=%wide.region_8.9_spmd.clone.clone, body=%wide.region_0.8_spmd.clone.clone.sunk | while | flops 1863155840 | bytes 82389584 | solution.py:133
  4.4 1.2 gather_fusion
  6.8 4.3 %collective-permute-start.1 = (bf16[2,256,512]{2,1,0:T(8,128)(2,1)S(1)}, bf16[2,256,512]{2,1,0:T(8,128)(2,1)S(1)}, u32[]{:S(2)}, u32[]{:S(2)}) collective-permute-start(bf16[2,256,512]{2,1,0:T(8,128)(2,1)S(1)} %pad_maximum_fusion.4), channel_id=1, source_target_pairs={{0,1},{1,2},{2,3},{3,4},{4,5},{5,6},{6,7},{7,8},{8,9},{9,10},{10,1... | collective-permute-start | bytes 1572872 | tf_op jit(solution)/shard_map/while/body/eval_jaxpr/ppermute | solution.py:21
  11.1 1.9 %collective-permute-start = (bf16[2,256,512]{2,1,0:T(8,128)(2,1)S(1)}, bf16[2,256,512]{2,1,0:T(8,128)(2,1)S(1)}, u32[]{:S(2)}, u32[]{:S(2)}) collective-permute-start(bf16[2,256,512]{2,1,0:T(8,128)(2,1)S(1)} %pad_maximum_fusion.4), channel_id=1, source_target_pairs={{1,0},{2,1},{3,2},{4,3},{5,4},{6,5},{7,6},{8,7},{9,8},{10,9},{11,1... | collective-permute-start | bytes 1572872 | tf_op jit(solution)/shard_map/while/body/eval_jaxpr/ppermute | solution.py:23
  14.1 1.1 reshape.279
  15.2 6.8 %collective-permute-done.1 = bf16[2,256,512]{2,1,0:T(8,128)(2,1)S(1)} collective-permute-done((bf16[2,256,512]{2,1,0:T(8,128)(2,1)S(1)}, bf16[2,256,512]{2,1,0:T(8,128)(2,1)S(1)}, u32[]{:S(2)}, u32[]{:S(2)}) %collective-permute-start.1) | collective-permute-done | bytes 524320 | tf_op jit(solution)/shard_map/while/body/eval_jaxpr/ppermute | solution.py:21
  22.0 9.3 %collective-permute-done = bf16[2,256,512]{2,1,0:T(8,128)(2,1)S(1)} collective-permute-done((bf16[2,256,512]{2,1,0:T(8,128)(2,1)S(1)}, bf16[2,256,512]{2,1,0:T(8,128)(2,1)S(1)}, u32[]{:S(2)}, u32[]{:S(2)}) %collective-permute-start) | collective-permute-done | bytes 524320 | tf_op jit(solution)/shard_map/while/body/eval_jaxpr/ppermute | solution.py:23
  31.4 1.0 fusion.168
  33.2 1.0 copy.82
  35.4 1.5 reshape.278
  37.7 1.0 copy.84
  41.2 1.2 fusion.171
  44.4 7.8 %bitcast_dynamic-update-slice_fusion.2 = (bf16[2,256,512]{2,1,0:T(8,128)(2,1)S(1)}, bf16[256,512]{1,0:T(8,128)(2,1)S(1)}) fusion(bf16[2,256,512]{2,1,0:T(8,128)(2,1)S(1)} %copy-done.7, s32[]{:T(128)S(6)} %min.27, f32[256,512]{1,0:T(8,128)S(1)} %get-tuple-element.644, bf16[1,2048,512]{2,1,0:T(8,128)(2,1)} %get-tuple-element.697, ...), kind=kOutput, calls=%fused_computation.100.clone.1 | convolution fusion | flops 1108475904 | bytes 5769220 | tf_op jit(solution)/shard_map/while/body/eval_jaxpr/dot_general | solution.py:112
  52.2 1.3 collective-permute-start.2
  53.5 2.5 %collective-permute-done.2 = bf16[256,512]{1,0:T(8,128)(2,1)S(1)} collective-permute-done((bf16[256,512]{1,0:T(8,128)(2,1)S(1)}, bf16[256,512]{1,0:T(8,128)(2,1)S(1)}, u32[]{:S(2)}, u32[]{:S(2)}) %collective-permute-start.2) | collective-permute-done | bytes 262176 | tf_op jit(solution)/shard_map/while/body/eval_jaxpr/ppermute | solution.py:33
  56.9 1.2 gather_fusion
  59.3 1.9 %collective-permute-start.1 = (bf16[2,256,512]{2,1,0:T(8,128)(2,1)S(1)}, bf16[2,256,512]{2,1,0:T(8,128)(2,1)S(1)}, u32[]{:S(2)}, u32[]{:S(2)}) collective-permute-start(bf16[2,256,512]{2,1,0:T(8,128)(2,1)S(1)} %pad_maximum_fusion.4), channel_id=1, source_target_pairs={{0,1},{1,2},{2,3},{3,4},{4,5},{5,6},{6,7},{7,8},{8,9},{9,10},{10,1... | collective-permute-start | bytes 1572872 | tf_op jit(solution)/shard_map/while/body/eval_jaxpr/ppermute | solution.py:21
  61.2 3.4 %collective-permute-start = (bf16[2,256,512]{2,1,0:T(8,128)(2,1)S(1)}, bf16[2,256,512]{2,1,0:T(8,128)(2,1)S(1)}, u32[]{:S(2)}, u32[]{:S(2)}) collective-permute-start(bf16[2,256,512]{2,1,0:T(8,128)(2,1)S(1)} %pad_maximum_fusion.4), channel_id=1, source_target_pairs={{1,0},{2,1},{3,2},{4,3},{5,4},{6,5},{7,6},{8,7},{9,8},{10,9},{11,1... | collective-permute-start | bytes 1572872 | tf_op jit(solution)/shard_map/while/body/eval_jaxpr/ppermute | solution.py:23
  65.6 1.1 reshape.279
  66.7 7.8 %collective-permute-done.1 = bf16[2,256,512]{2,1,0:T(8,128)(2,1)S(1)} collective-permute-done((bf16[2,256,512]{2,1,0:T(8,128)(2,1)S(1)}, bf16[2,256,512]{2,1,0:T(8,128)(2,1)S(1)}, u32[]{:S(2)}, u32[]{:S(2)}) %collective-permute-start.1) | collective-permute-done | bytes 524320 | tf_op jit(solution)/shard_map/while/body/eval_jaxpr/ppermute | solution.py:21
  74.5 7.4 %collective-permute-done = bf16[2,256,512]{2,1,0:T(8,128)(2,1)S(1)} collective-permute-done((bf16[2,256,512]{2,1,0:T(8,128)(2,1)S(1)}, bf16[2,256,512]{2,1,0:T(8,128)(2,1)S(1)}, u32[]{:S(2)}, u32[]{:S(2)}) %collective-permute-start) | collective-permute-done | bytes 524320 | tf_op jit(solution)/shard_map/while/body/eval_jaxpr/ppermute | solution.py:23
  82.0 1.0 fusion.168
  83.8 1.0 copy.82
  86.0 1.5 reshape.278
  88.3 1.0 copy.84
  91.8 1.2 fusion.171
  93.0 0.9 fusion.172
  95.0 7.8 %bitcast_dynamic-update-slice_fusion.2 = (bf16[2,256,512]{2,1,0:T(8,128)(2,1)S(1)}, bf16[256,512]{1,0:T(8,128)(2,1)S(1)}) fusion(bf16[2,256,512]{2,1,0:T(8,128)(2,1)S(1)} %copy-done.7, s32[]{:T(128)S(6)} %min.27, f32[256,512]{1,0:T(8,128)S(1)} %get-tuple-element.644, bf16[1,2048,512]{2,1,0:T(8,128)(2,1)} %get-tuple-element.697, ...), kind=kOutput, calls=%fused_computation.100.clone.1 | convolution fusion | flops 1108475904 | bytes 5769220 | tf_op jit(solution)/shard_map/while/body/eval_jaxpr/dot_general | solution.py:112
  102.8 1.3 collective-permute-start.2
  104.1 2.1 %collective-permute-done.2 = bf16[256,512]{1,0:T(8,128)(2,1)S(1)} collective-permute-done((bf16[256,512]{1,0:T(8,128)(2,1)S(1)}, bf16[256,512]{1,0:T(8,128)(2,1)S(1)}, u32[]{:S(2)}, u32[]{:S(2)}) %collective-permute-start.2) | collective-permute-done | bytes 262176 | tf_op jit(solution)/shard_map/while/body/eval_jaxpr/ppermute | solution.py:33
  107.1 1.2 gather_fusion
  109.5 1.9 %collective-permute-start.1 = (bf16[2,256,512]{2,1,0:T(8,128)(2,1)S(1)}, bf16[2,256,512]{2,1,0:T(8,128)(2,1)S(1)}, u32[]{:S(2)}, u32[]{:S(2)}) collective-permute-start(bf16[2,256,512]{2,1,0:T(8,128)(2,1)S(1)} %pad_maximum_fusion.4), channel_id=1, source_target_pairs={{0,1},{1,2},{2,3},{3,4},{4,5},{5,6},{6,7},{7,8},{8,9},{9,10},{10,1... | collective-permute-start | bytes 1572872 | tf_op jit(solution)/shard_map/while/body/eval_jaxpr/ppermute | solution.py:21
  111.4 3.4 %collective-permute-start = (bf16[2,256,512]{2,1,0:T(8,128)(2,1)S(1)}, bf16[2,256,512]{2,1,0:T(8,128)(2,1)S(1)}, u32[]{:S(2)}, u32[]{:S(2)}) collective-permute-start(bf16[2,256,512]{2,1,0:T(8,128)(2,1)S(1)} %pad_maximum_fusion.4), channel_id=1, source_target_pairs={{1,0},{2,1},{3,2},{4,3},{5,4},{6,5},{7,6},{8,7},{9,8},{10,9},{11,1... | collective-permute-start | bytes 1572872 | tf_op jit(solution)/shard_map/while/body/eval_jaxpr/ppermute | solution.py:23
  115.9 1.1 reshape.279
  116.9 7.8 %collective-permute-done.1 = bf16[2,256,512]{2,1,0:T(8,128)(2,1)S(1)} collective-permute-done((bf16[2,256,512]{2,1,0:T(8,128)(2,1)S(1)}, bf16[2,256,512]{2,1,0:T(8,128)(2,1)S(1)}, u32[]{:S(2)}, u32[]{:S(2)}) %collective-permute-start.1) | collective-permute-done | bytes 524320 | tf_op jit(solution)/shard_map/while/body/eval_jaxpr/ppermute | solution.py:21
  124.7 7.4 %collective-permute-done = bf16[2,256,512]{2,1,0:T(8,128)(2,1)S(1)} collective-permute-done((bf16[2,256,512]{2,1,0:T(8,128)(2,1)S(1)}, bf16[2,256,512]{2,1,0:T(8,128)(2,1)S(1)}, u32[]{:S(2)}, u32[]{:S(2)}) %collective-permute-start) | collective-permute-done | bytes 524320 | tf_op jit(solution)/shard_map/while/body/eval_jaxpr/ppermute | solution.py:23
  132.2 1.0 fusion.168
  134.0 1.0 copy.82
  136.3 1.5 reshape.278
  138.5 1.0 copy.84
  142.0 1.2 fusion.171
  143.2 0.9 fusion.172
  145.2 7.8 %bitcast_dynamic-update-slice_fusion.2 = (bf16[2,256,512]{2,1,0:T(8,128)(2,1)S(1)}, bf16[256,512]{1,0:T(8,128)(2,1)S(1)}) fusion(bf16[2,256,512]{2,1,0:T(8,128)(2,1)S(1)} %copy-done.7, s32[]{:T(128)S(6)} %min.27, f32[256,512]{1,0:T(8,128)S(1)} %get-tuple-element.644, bf16[1,2048,512]{2,1,0:T(8,128)(2,1)} %get-tuple-element.697, ...), kind=kOutput, calls=%fused_computation.100.clone.1 | convolution fusion | flops 1108475904 | bytes 5769220 | tf_op jit(solution)/shard_map/while/body/eval_jaxpr/dot_general | solution.py:112
  153.1 1.3 collective-permute-start.2
  154.4 2.1 %collective-permute-done.2 = bf16[256,512]{1,0:T(8,128)(2,1)S(1)} collective-permute-done((bf16[256,512]{1,0:T(8,128)(2,1)S(1)}, bf16[256,512]{1,0:T(8,128)(2,1)S(1)}, u32[]{:S(2)}, u32[]{:S(2)}) %collective-permute-start.2) | collective-permute-done | bytes 262176 | tf_op jit(solution)/shard_map/while/body/eval_jaxpr/ppermute | solution.py:33
  156.5 3.6 %all-to-all-start = ((bf16[2,256,512]{2,1,0:T(8,128)(2,1)}), bf16[2,256,512]{2,1,0:T(8,128)(2,1)S(1)}, u32[]{:S(2)}, u32[]{:S(2)}) async-start(bf16[2,256,512]{2,1,0:T(8,128)(2,1)} %get-tuple-element.409), calls=%async_computation | async-start | bytes 1048576 | tf_op jit(solution)/shard_map/all_to_all | solution.py:135
  160.1 1.3 dynamic_slice.44
  (171 shorter events, 31.9 us)
Async XLA Ops:
  3.5 3.1 %copy-start.5 = (bf16[2,256,512]{2,1,0:T(8,128)(2,1)}, bf16[2,256,512]{2,1,0:T(8,128)(2,1)S(1)}, u32[]{:S(2)}) copy-start(bf16[2,256,512]{2,1,0:T(8,128)(2,1)S(1)} %get-tuple-element.688) | copy-start | bytes 1572868 | tf_op jit(solution)/shard_map/while
  3.5 2.4 %copy-start.3 = (bf16[1,512,1536]{2,1,0:T(8,128)(2,1)S(1)}, bf16[1,512,1536]{2,1,0:T(8,128)(2,1)}, u32[]{:S(2)}) copy-start(bf16[1,512,1536]{2,1,0:T(8,128)(2,1)} %get-tuple-element.691) | copy-start | bytes 4718596 | tf_op jit(solution)/shard_map/while
  6.0 7.1 %copy-start.10 = (s32[2,2,3]{2,1,0:T(2,128)S(1)}, s32[2,2,3]{2,1,0:T(2,128)}, u32[]{:S(2)}) copy-start(s32[2,2,3]{2,1,0:T(2,128)} %get-tuple-element.692) | copy-start | bytes 148 | tf_op jit(solution)/shard_map/while
  6.0 7.2 %copy-start.9 = (s32[2,256]{1,0:T(2,128)S(1)}, s32[2,256]{1,0:T(2,128)}, u32[]{:S(2)}) copy-start(s32[2,256]{1,0:T(2,128)} %get-tuple-element.694) | copy-start | bytes 6148 | tf_op jit(solution)/shard_map/while
  6.8 15.2 %collective-permute-start.1 = (bf16[2,256,512]{2,1,0:T(8,128)(2,1)S(1)}, bf16[2,256,512]{2,1,0:T(8,128)(2,1)S(1)}, u32[]{:S(2)}, u32[]{:S(2)}) collective-permute-start(bf16[2,256,512]{2,1,0:T(8,128)(2,1)S(1)} %pad_maximum_fusion.4), channel_id=1, source_target_pairs={{0,1},{1,2},{2,3},{3,4},{4,5},{5,6},{6,7},{7,8},{8,9},{9,10},{10,1... | collective-permute-start | bytes 1572872 | tf_op jit(solution)/shard_map/while/body/eval_jaxpr/ppermute | solution.py:21
  11.1 20.1 %collective-permute-start = (bf16[2,256,512]{2,1,0:T(8,128)(2,1)S(1)}, bf16[2,256,512]{2,1,0:T(8,128)(2,1)S(1)}, u32[]{:S(2)}, u32[]{:S(2)}) collective-permute-start(bf16[2,256,512]{2,1,0:T(8,128)(2,1)S(1)} %pad_maximum_fusion.4), channel_id=1, source_target_pairs={{1,0},{2,1},{3,2},{4,3},{5,4},{6,5},{7,6},{8,7},{9,8},{10,9},{11,1... | collective-permute-start | bytes 1572872 | tf_op jit(solution)/shard_map/while/body/eval_jaxpr/ppermute | solution.py:23
  35.4 1.5 copy-start.1
  39.4 1.1 copy-start
  39.4 1.3 copy-start.2
  42.4 1.2 copy-start.4
  43.3 1.1 copy-start.7
  44.4 11.7 %copy-start.6 = (bf16[2,256,512]{2,1,0:T(8,128)(2,1)S(1)}, bf16[2,256,512]{2,1,0:T(8,128)(2,1)}, u32[]{:S(2)}) copy-start(bf16[2,256,512]{2,1,0:T(8,128)(2,1)} %copy-done.5) | copy-start | bytes 1572868 | tf_op jit(solution)/shard_map/while
  52.2 3.8 %copy-start.8 = (bf16[2,256,512]{2,1,0:T(8,128)(2,1)}, bf16[2,256,512]{2,1,0:T(8,128)(2,1)S(1)}, u32[]{:S(2)}) copy-start(bf16[2,256,512]{2,1,0:T(8,128)(2,1)S(1)} %get-tuple-element.686) | copy-start | bytes 1572868 | tf_op jit(solution)/shard_map/while
  52.2 3.8 %collective-permute-start.2 = (bf16[256,512]{1,0:T(8,128)(2,1)S(1)}, bf16[256,512]{1,0:T(8,128)(2,1)S(1)}, u32[]{:S(2)}, u32[]{:S(2)}) collective-permute-start(bf16[256,512]{1,0:T(8,128)(2,1)S(1)} %get-tuple-element.646), channel_id=1, source_target_pairs={{0,256},{1,257},{2,258},{3,259},{4,260},{5,261},{6,262},{7,263},{8... | collective-permute-start | bytes 786440 | tf_op jit(solution)/shard_map/while/body/eval_jaxpr/ppermute | solution.py:33
  56.0 3.1 %copy-start.5 = (bf16[2,256,512]{2,1,0:T(8,128)(2,1)}, bf16[2,256,512]{2,1,0:T(8,128)(2,1)S(1)}, u32[]{:S(2)}) copy-start(bf16[2,256,512]{2,1,0:T(8,128)(2,1)S(1)} %get-tuple-element.688) | copy-start | bytes 1572868 | tf_op jit(solution)/shard_map/while
  56.0 2.4 %copy-start.3 = (bf16[1,512,1536]{2,1,0:T(8,128)(2,1)S(1)}, bf16[1,512,1536]{2,1,0:T(8,128)(2,1)}, u32[]{:S(2)}) copy-start(bf16[1,512,1536]{2,1,0:T(8,128)(2,1)} %get-tuple-element.691) | copy-start | bytes 4718596 | tf_op jit(solution)/shard_map/while
  58.5 6.1 %copy-start.10 = (s32[2,2,3]{2,1,0:T(2,128)S(1)}, s32[2,2,3]{2,1,0:T(2,128)}, u32[]{:S(2)}) copy-start(s32[2,2,3]{2,1,0:T(2,128)} %get-tuple-element.692) | copy-start | bytes 148 | tf_op jit(solution)/shard_map/while
  58.5 6.2 %copy-start.9 = (s32[2,256]{1,0:T(2,128)S(1)}, s32[2,256]{1,0:T(2,128)}, u32[]{:S(2)}) copy-start(s32[2,256]{1,0:T(2,128)} %get-tuple-element.694) | copy-start | bytes 6148 | tf_op jit(solution)/shard_map/while
  59.3 15.2 %collective-permute-start.1 = (bf16[2,256,512]{2,1,0:T(8,128)(2,1)S(1)}, bf16[2,256,512]{2,1,0:T(8,128)(2,1)S(1)}, u32[]{:S(2)}, u32[]{:S(2)}) collective-permute-start(bf16[2,256,512]{2,1,0:T(8,128)(2,1)S(1)} %pad_maximum_fusion.4), channel_id=1, source_target_pairs={{0,1},{1,2},{2,3},{3,4},{4,5},{5,6},{6,7},{7,8},{8,9},{9,10},{10,1... | collective-permute-start | bytes 1572872 | tf_op jit(solution)/shard_map/while/body/eval_jaxpr/ppermute | solution.py:21
  61.2 20.7 %collective-permute-start = (bf16[2,256,512]{2,1,0:T(8,128)(2,1)S(1)}, bf16[2,256,512]{2,1,0:T(8,128)(2,1)S(1)}, u32[]{:S(2)}, u32[]{:S(2)}) collective-permute-start(bf16[2,256,512]{2,1,0:T(8,128)(2,1)S(1)} %pad_maximum_fusion.4), channel_id=1, source_target_pairs={{1,0},{2,1},{3,2},{4,3},{5,4},{6,5},{7,6},{8,7},{9,8},{10,9},{11,1... | collective-permute-start | bytes 1572872 | tf_op jit(solution)/shard_map/while/body/eval_jaxpr/ppermute | solution.py:23
  86.0 1.5 copy-start.1
  90.0 1.1 copy-start
  90.0 1.3 copy-start.2
  93.0 1.2 copy-start.4
  93.9 1.1 copy-start.7
  95.0 11.3 %copy-start.6 = (bf16[2,256,512]{2,1,0:T(8,128)(2,1)S(1)}, bf16[2,256,512]{2,1,0:T(8,128)(2,1)}, u32[]{:S(2)}) copy-start(bf16[2,256,512]{2,1,0:T(8,128)(2,1)} %copy-done.5) | copy-start | bytes 1572868 | tf_op jit(solution)/shard_map/while
  102.8 3.4 %copy-start.8 = (bf16[2,256,512]{2,1,0:T(8,128)(2,1)}, bf16[2,256,512]{2,1,0:T(8,128)(2,1)S(1)}, u32[]{:S(2)}) copy-start(bf16[2,256,512]{2,1,0:T(8,128)(2,1)S(1)} %get-tuple-element.686) | copy-start | bytes 1572868 | tf_op jit(solution)/shard_map/while
  102.8 3.4 %collective-permute-start.2 = (bf16[256,512]{1,0:T(8,128)(2,1)S(1)}, bf16[256,512]{1,0:T(8,128)(2,1)S(1)}, u32[]{:S(2)}, u32[]{:S(2)}) collective-permute-start(bf16[256,512]{1,0:T(8,128)(2,1)S(1)} %get-tuple-element.646), channel_id=1, source_target_pairs={{0,256},{1,257},{2,258},{3,259},{4,260},{5,261},{6,262},{7,263},{8... | collective-permute-start | bytes 786440 | tf_op jit(solution)/shard_map/while/body/eval_jaxpr/ppermute | solution.py:33
  106.3 3.1 %copy-start.5 = (bf16[2,256,512]{2,1,0:T(8,128)(2,1)}, bf16[2,256,512]{2,1,0:T(8,128)(2,1)S(1)}, u32[]{:S(2)}) copy-start(bf16[2,256,512]{2,1,0:T(8,128)(2,1)S(1)} %get-tuple-element.688) | copy-start | bytes 1572868 | tf_op jit(solution)/shard_map/while
  106.3 2.4 %copy-start.3 = (bf16[1,512,1536]{2,1,0:T(8,128)(2,1)S(1)}, bf16[1,512,1536]{2,1,0:T(8,128)(2,1)}, u32[]{:S(2)}) copy-start(bf16[1,512,1536]{2,1,0:T(8,128)(2,1)} %get-tuple-element.691) | copy-start | bytes 4718596 | tf_op jit(solution)/shard_map/while
  108.7 6.1 %copy-start.10 = (s32[2,2,3]{2,1,0:T(2,128)S(1)}, s32[2,2,3]{2,1,0:T(2,128)}, u32[]{:S(2)}) copy-start(s32[2,2,3]{2,1,0:T(2,128)} %get-tuple-element.692) | copy-start | bytes 148 | tf_op jit(solution)/shard_map/while
  108.7 6.2 %copy-start.9 = (s32[2,256]{1,0:T(2,128)S(1)}, s32[2,256]{1,0:T(2,128)}, u32[]{:S(2)}) copy-start(s32[2,256]{1,0:T(2,128)} %get-tuple-element.694) | copy-start | bytes 6148 | tf_op jit(solution)/shard_map/while
  109.5 15.2 %collective-permute-start.1 = (bf16[2,256,512]{2,1,0:T(8,128)(2,1)S(1)}, bf16[2,256,512]{2,1,0:T(8,128)(2,1)S(1)}, u32[]{:S(2)}, u32[]{:S(2)}) collective-permute-start(bf16[2,256,512]{2,1,0:T(8,128)(2,1)S(1)} %pad_maximum_fusion.4), channel_id=1, source_target_pairs={{0,1},{1,2},{2,3},{3,4},{4,5},{5,6},{6,7},{7,8},{8,9},{9,10},{10,1... | collective-permute-start | bytes 1572872 | tf_op jit(solution)/shard_map/while/body/eval_jaxpr/ppermute | solution.py:21
  111.4 20.7 %collective-permute-start = (bf16[2,256,512]{2,1,0:T(8,128)(2,1)S(1)}, bf16[2,256,512]{2,1,0:T(8,128)(2,1)S(1)}, u32[]{:S(2)}, u32[]{:S(2)}) collective-permute-start(bf16[2,256,512]{2,1,0:T(8,128)(2,1)S(1)} %pad_maximum_fusion.4), channel_id=1, source_target_pairs={{1,0},{2,1},{3,2},{4,3},{5,4},{6,5},{7,6},{8,7},{9,8},{10,9},{11,1... | collective-permute-start | bytes 1572872 | tf_op jit(solution)/shard_map/while/body/eval_jaxpr/ppermute | solution.py:23
  136.2 1.5 copy-start.1
  140.2 1.1 copy-start
  140.2 1.3 copy-start.2
  143.2 1.2 copy-start.4
  144.1 1.1 copy-start.7
  145.2 11.3 %copy-start.6 = (bf16[2,256,512]{2,1,0:T(8,128)(2,1)S(1)}, bf16[2,256,512]{2,1,0:T(8,128)(2,1)}, u32[]{:S(2)}) copy-start(bf16[2,256,512]{2,1,0:T(8,128)(2,1)} %copy-done.5) | copy-start | bytes 1572868 | tf_op jit(solution)/shard_map/while
  153.0 3.4 %copy-start.8 = (bf16[2,256,512]{2,1,0:T(8,128)(2,1)}, bf16[2,256,512]{2,1,0:T(8,128)(2,1)S(1)}, u32[]{:S(2)}) copy-start(bf16[2,256,512]{2,1,0:T(8,128)(2,1)S(1)} %get-tuple-element.686) | copy-start | bytes 1572868 | tf_op jit(solution)/shard_map/while
  153.1 3.4 %collective-permute-start.2 = (bf16[256,512]{1,0:T(8,128)(2,1)S(1)}, bf16[256,512]{1,0:T(8,128)(2,1)S(1)}, u32[]{:S(2)}, u32[]{:S(2)}) collective-permute-start(bf16[256,512]{1,0:T(8,128)(2,1)S(1)} %get-tuple-element.646), channel_id=1, source_target_pairs={{0,256},{1,257},{2,258},{3,259},{4,260},{5,261},{6,262},{7,263},{8... | collective-permute-start | bytes 786440 | tf_op jit(solution)/shard_map/while/body/eval_jaxpr/ppermute | solution.py:33
  156.5 5.5 %all-to-all-start = ((bf16[2,256,512]{2,1,0:T(8,128)(2,1)}), bf16[2,256,512]{2,1,0:T(8,128)(2,1)S(1)}, u32[]{:S(2)}, u32[]{:S(2)}) async-start(bf16[2,256,512]{2,1,0:T(8,128)(2,1)} %get-tuple-element.409), calls=%async_computation | async-start | bytes 1048576 | tf_op jit(solution)/shard_map/all_to_all | solution.py:135
where the time goes:
time: 163 us
  waiting for transfers between devices  53.2 us (33%)
  local copies, waits for them, and re-layouts  39.9 us (24%)
  matrix products  31 us (19%)
  starting transfers between devices  24.3 us (15%)
  other arithmetic  10.8 us (7%)
  blocking collectives  2.68 us (2%)
    ppermute x3, waiting for transfers between devices, with_halo(): lax.ppermute(head, axis, [((i + 1) % count, i) for i in range(ends)])  24 us
    dot_general x3, matrix products, run_block(): jnp.dot(hidden, w_down[0], preferred_element_type=jnp.float32)  23.5 us
    ppermute x3, waiting for transfers between devices, with_halo(): lax.ppermute(tail, axis, [(i, (i + 1) % count) for i in range(ends)])  22.5 us
    ppermute x3, starting transfers between devices, with_halo(): lax.ppermute(head, axis, [((i + 1) % count, i) for i in range(ends)])  8.64 us
    ppermute x3, starting transfers between devices, with_halo(): lax.ppermute(tail, axis, [(i, (i + 1) % count) for i in range(ends)])  8.17 us
    ppermute x3, waiting for transfers between devices, passed_along(): return lax.ppermute(value, axis, pairs)  6.77 us
    squeeze x6, local copies, waits for them, and re-layouts, attend(): near_values.reshape(-1, patch_rows, HEADS, head_width)[local_links]  5.29 us
    squeeze x6, local copies, waits for them, and re-layouts, attend(): key_part = near_keys.reshape(-1, patch_rows, HEADS, head_width)[local_links]  5.29 us
  transfers between devices with their start and end apart: 10, of which 9 were waited for; matrix products, arithmetic and copies ran while one was open for 5% of the time, Pallas kernels for 0%

commit v1 on v0

v1 whole, which is shorter than its diff:
```python
import functools

import jax
import jax.numpy as jnp
from jax import lax
from jax.experimental import pallas as pl
from jax.experimental.pallas import tpu as pltpu
from jax.sharding import PartitionSpec as P

HEADS = 8
HEAD = 64
D = 512
PATCH = 128
LINKS = 3
PAIRS = HEADS // 2
EPS = 1e-05
BF16 = jnp.bfloat16
F32 = jnp.float32

QKV, OUT, UP, DOWN, SLOTS = 0, 3, 4, 8, 12


def dot(a, b):
    return jnp.dot(a, b, preferred_element_type=F32)


def normalize(values):
    center = jnp.mean(values, axis=-1, keepdims=True)
    shifted = values - center
    spread = jnp.mean(shifted * shifted, axis=-1, keepdims=True)
    return (shifted * lax.rsqrt(spread + EPS)).astype(BF16)


def gelu(x):
    return 0.5 * x * (1.0 + lax.erf(x * (0.5**0.5)))


def arrange_kernel(
    hits_hbm, order_hbm, w_qkv, w_out, w_up, w_down, ordered, packed, hits, order, sem
):
    event = lax.axis_index("section")
    pairs = [(hits_hbm.at[0], hits), (order_hbm.at[event], order)]
    for i in range(3):
        pairs.append((w_qkv.at[0, :, pl.ds(i * D, D)], packed.at[QKV + i]))
    pairs.append((w_out.at[0], packed.at[OUT]))
    for i in range(4):
        pairs.append((w_up.at[0, :, pl.ds(i * D, D)], packed.at[UP + i]))
    for i in range(4):
        pairs.append((w_down.at[0, pl.ds(i * D, D), :], packed.at[DOWN + i]))
    copies = [pltpu.make_async_copy(a, b, sem.at[i]) for i, (a, b) in enumerate(pairs)]
    for copy in copies:
        copy.start()
    copies[0].wait()
    copies[1].wait()
    rows = hits.shape[0]
    source_row = lax.broadcasted_iota(jnp.int32, (rows, rows), 0)
    chosen = jnp.where(source_row == order[...], 1.0, 0.0).T.astype(BF16)
    ordered[...] = dot(chosen, hits[...]).astype(BF16)
    for copy in copies[2:]:
        copy.wait()


def arrange(hits, order, *weights):
    rows = hits.shape[1]
    vmem = pl.BlockSpec(memory_space=pltpu.VMEM)
    args = [pltpu.with_memory_space_constraint(a, pltpu.HBM) for a in (hits, order, *weights)]
    return pl.pallas_call(
        arrange_kernel,
        name="arrange",
        out_shape=(
            jax.ShapeDtypeStruct((rows, D), BF16),
            jax.ShapeDtypeStruct((SLOTS, D, D), BF16),
        ),
        in_specs=[pl.BlockSpec(memory_space=pltpu.HBM)] * 6,
        out_specs=(vmem, vmem),
        scratch_shapes=[
            pltpu.VMEM((rows, D), BF16),
            pltpu.VMEM((1, rows), jnp.int32),
            pltpu.SemaphoreType.DMA((SLOTS + 2,)),
        ],
        compiler_params=pltpu.CompilerParams(vmem_limit_bytes=20 << 20),
        cost_estimate=pl.CostEstimate(
            flops=2 * rows * rows * D, bytes_accessed=13 << 20, transcendentals=0
        ),
    )(*args)


def fetch(block, own, came, weights, sem, slots):
    section = lax.axis_index("section")

    def copies(source):
        return [
            pltpu.make_async_copy(source.at[slot], weights.at[at], sem.at[at])
            for at, slot in enumerate(slots)
        ]

    @pl.when(section == block)
    def _():
        for copy in copies(own):
            copy.start()

    @pl.when(section != block)
    def _():
        for copy in copies(came):
            copy.start()

    waits = dict(zip(slots, copies(own)))
    place = {slot: at for at, slot in enumerate(slots)}

    def weight(slot):
        if waits[slot] is not None:
            waits[slot].wait()
            waits[slot] = None
        return weights[place[slot]]

    return weight


def project_kernel(block, state, own, came, mixed, weights, sem):
    weight = fetch(block, own, came, weights, sem, (QKV, QKV + 1, QKV + 2))
    normed = normalize(state[...].astype(F32))
    for i in range(3):
        part = dot(normed, weight(QKV + i)).astype(BF16)
        if i == 0:
            part = part * jnp.asarray(HEAD**-0.5, BF16)
        mixed[:, i * D : (i + 1) * D] = part


def project(block, state, own, came):
    rows = state.shape[0]
    any_space = pl.BlockSpec(memory_space=pl.ANY)
    vmem = pl.BlockSpec(memory_space=pltpu.VMEM)
    return pl.pallas_call(
        functools.partial(project_kernel, block),
        name=f"project_{block}",
        out_shape=jax.ShapeDtypeStruct((rows, 3 * D), BF16),
        in_specs=[vmem, any_space, any_space],
        out_specs=vmem,
        scratch_shapes=[pltpu.VMEM((3, D, D), BF16), pltpu.SemaphoreType.DMA((3,))],
        compiler_params=pltpu.CompilerParams(vmem_limit_bytes=10 << 20),
        cost_estimate=pl.CostEstimate(
            flops=6 * rows * D * D, bytes_accessed=3 << 20, transcendentals=0
        ),
    )(state, own, came)


def block_kernel(
    block,
    last,
    links,
    counts,
    state,
    mixed,
    near_a,
    near_b,
    own,
    came,
    result,
    weights,
    keys,
    values,
    attended,
    sem,
):
    weight = fetch(block, own, came, weights, sem, tuple(range(QKV + 1, SLOTS)))
    event = lax.axis_index("section")
    region = lax.axis_index("region")
    regions = counts.shape[1]
    rows = state.shape[0]
    patches = rows // PATCH
    even = lax.rem(region, 2) == 0
    region_a = jnp.where(even, region + 1, region - 1)
    region_b = jnp.where(even, region - 1, region + 1)
    lane = lax.broadcasted_iota(jnp.int32, (1, 2 * HEAD), 1)
    low = lane < HEAD
    ones_low = jnp.broadcast_to(jnp.where(low, 1.0, 0.0).astype(BF16), (PATCH, PATCH))
    ones_high = jnp.broadcast_to(jnp.where(low, 0.0, 1.0).astype(BF16), (PATCH, PATCH))

    def spread(slot, key_rows, value_rows):
        for pair in range(PAIRS):
            k = key_rows[:, pair * 128 : (pair + 1) * 128]
            v = value_rows[:, pair * 128 : (pair + 1) * 128]
            keys[slot, pair, 0:PATCH, :] = k * ones_low
            keys[slot, pair, PATCH : 2 * PATCH, :] = k * ones_high
            values[slot, pair, 0:PATCH, 0:128] = v * ones_low
            values[slot, pair, PATCH : 2 * PATCH, 0:128] = v * ones_high
            values[slot, pair, 0:PATCH, 128:256] = ones_low
            values[slot, pair, PATCH : 2 * PATCH, 128:256] = ones_high

    for patch in range(patches):
        here = pl.ds(patch * PATCH, PATCH)
        spread(patch, mixed[here, D : 2 * D], mixed[here, 2 * D : 3 * D])
    for base, near in ((patches, near_a), (2 * patches, near_b)):
        normed = normalize(near[...].astype(F32))
        key_rows = dot(normed, weight(QKV + 1)).astype(BF16)
        value_rows = dot(normed, weight(QKV + 2)).astype(BF16)
        for patch in range(patches):
            cut = slice(patch * PATCH, (patch + 1) * PATCH)
            spread(base + patch, key_rows[cut], value_rows[cut])

    count_own = counts[event, region]
    count_a = counts[event, jnp.clip(region_a, 0, regions - 1)]
    count_b = counts[event, jnp.clip(region_b, 0, regions - 1)]
    key_lane = jnp.bitwise_and(lax.broadcasted_iota(jnp.int32, (PATCH, 2 * PATCH), 1), PATCH - 1)
    for patch in range(patches):
        slots, valid = [], []
        for link in range(LINKS):
            linked = links[event, patch, link]
            owner = lax.div(linked, patches)
            half = lax.rem(linked, patches)
            base = jnp.where(owner == region, 0, jnp.where(owner == region_a, 1, 2))
            count = jnp.where(base == 0, count_own, jnp.where(base == 1, count_a, count_b))
            slots.append(base * patches + half)
            valid.append(key_lane < count - half * PATCH)
        here = pl.ds(patch * PATCH, PATCH)
        for pair in range(PAIRS):
            across = pl.ds(pair * 128, 128)
            query = mixed[here, across]
            scores = [
                jnp.where(
                    valid[link],
                    lax.dot_general(
                        query,
                        keys[slots[link], pair],
                        (((1,), (1,)), ((), ())),
                        preferred_element_type=F32,
                    ),
                    -1e30,
                )
                for link in range(LINKS)
            ]
            top = functools.reduce(jnp.maximum, scores)
            top_low = jnp.max(top[:, :PATCH], axis=-1, keepdims=True)
            top_high = jnp.max(top[:, PATCH:], axis=-1, keepdims=True)
            total = None
            for link in range(LINKS):
                weighed = jnp.concatenate(
                    [
                        jnp.exp(scores[link][:, :PATCH] - top_low),
                        jnp.exp(scores[link][:, PATCH:] - top_high),
                    ],
                    axis=1,
                ).astype(BF16)
                part = dot(weighed, values[slots[link], pair])
                total = part if total is None else total + part
            attended[here, across] = (total[:, :128] / total[:, 128:]).astype(BF16)

    middle = (state[...].astype(F32) + dot(attended[...], weight(OUT))).astype(BF16)
    middle = middle.astype(F32)
    normed = normalize(middle)
    total = middle
    for part in range(4):
        hidden = gelu(dot(normed, weight(UP + part))).astype(BF16)
        total = total + dot(hidden, weight(DOWN + part))
    total = total.astype(BF16)
    if last:
        row = lax.broadcasted_iota(jnp.int32, (rows, D), 0)
        total = jnp.where(row < count_own, total.astype(F32), 0.0).astype(BF16)
    result[...] = total


def run_block(block, last, links, counts, state, mixed, near_a, near_b, own, came):
    rows = state.shape[0]
    patches = rows // PATCH
    any_space = pl.BlockSpec(memory_space=pl.ANY)
    vmem = pl.BlockSpec(memory_space=pltpu.VMEM)
    smem = pl.BlockSpec(memory_space=pltpu.SMEM)
    return pl.pallas_call(
        functools.partial(block_kernel, block, last),
        name=f"block_{block}",
        out_shape=jax.ShapeDtypeStruct((rows, D), BF16),
        in_specs=[smem, smem, vmem, vmem, vmem, vmem, any_space, any_space],
        out_specs=vmem,
        scratch_shapes=[
            pltpu.VMEM((SLOTS - 1, D, D), BF16),
            pltpu.VMEM((3 * patches, PAIRS, 2 * PATCH, 128), BF16),
            pltpu.VMEM((3 * patches, PAIRS, 2 * PATCH, 256), BF16),
            pltpu.VMEM((rows, D), BF16),
            pltpu.SemaphoreType.DMA((SLOTS - 1,)),
        ],
        compiler_params=pltpu.CompilerParams(vmem_limit_bytes=32 << 20),
        cost_estimate=pl.CostEstimate(
            flops=4 * 10**9, bytes_accessed=8 << 20, transcendentals=2 * 10**6
        ),
    )(links, counts, state, mixed, near_a, near_b, own, came)


def per_device(hits, order, links, counts, w_qkv, w_out, w_up, w_down):
    regions = counts.shape[1]
    pairs_a = [(i, i ^ 1) for i in range(regions)]
    pairs_b = []
    for i in range(1, regions - 1, 2):
        pairs_b += [(i, i + 1), (i + 1, i)]
    ordered, own = arrange(hits, order, w_qkv, w_out, w_up, w_down)
    came = lax.ppermute(own, "section", [(0, 1), (1, 0)])
    state = ordered
    for block in range(2):
        near_b = lax.ppermute(state, "region", pairs_b)
        near_a = lax.ppermute(state, "region", pairs_a)
        mixed = project(block, state, own, came)
        state = run_block(
            block, block == 1, links, counts, state, mixed, near_a, near_b, own, came
        )
    return state[None]


def solution(mesh):
    in_specs = (
        P("section", "region", None),
        P(None, "region", None),
        P(None, "region", None),
        P(),
        P("section", None, None),
        P("section", None, None),
        P("section", None, None),
        P("section", None, None),
    )
    out_specs = P("section", "region", None)
    return jax.shard_map(
        per_device, mesh=mesh, in_specs=in_specs, out_specs=out_specs, check_vma=False
    )
```

time: 163 us -> 52 us (0.32)
  the two profiles are of different devices: /device:TPU:255 before, /device:TPU:256 now
where the time goes in v1:
time: 52 us; the launch traced here: 51.8 us
  Pallas kernels  20.1 us (39%)
  starting transfers between devices  18.1 us (35%)
  waiting for transfers between devices  13.3 us (26%)
    pallas_call x2, Pallas kernels, run_block(): pl.pallas_call(functools.partial(block_kernel, block, last), name=f'block...  14.5 us
    ppermute x2, starting transfers between devices, per_device(): near_b = lax.ppermute(state, 'region', pairs_b)  12.4 us
    ppermute x2, waiting for transfers between devices, per_device(): near_b = lax.ppermute(state, 'region', pairs_b)  10.6 us
    ppermute x2, starting transfers between devices, per_device(): near_a = lax.ppermute(state, 'region', pairs_a)  3.84 us
    pallas_call x1, Pallas kernels, arrange(): pl.pallas_call(arrange_kernel, name='arrange', out_shape=(jax.ShapeDtypeS...  3.02 us
    pallas_call x2, Pallas kernels, project(): pl.pallas_call(functools.partial(project_kernel, block), name=f'project_{...  2.6 us
    ppermute x1, starting transfers between devices, per_device(): came = lax.ppermute(own, 'section', [(0, 1), (1, 0)])  1.92 us
    ppermute x1, waiting for transfers between devices, per_device(): came = lax.ppermute(own, 'section', [(0, 1), (1, 0)])  1.5 us
  transfers between devices with their start and end apart: 5, of which 5 were waited for; matrix products, arithmetic and copies ran while one was open for 0% of the time, Pallas kernels for 5%

profile of v1, /device:TPU:256, one launch (start us, length us, event | category | flops | bytes accessed | tf_op | source)
XLA Modules:
  0.0 51.8 jit_solution(12669700590664041522)
XLA Ops:
  0.0 3.0 %arrange.1 = (bf16[256,512]{1,0:T(8,128)(2,1)S(1)}, bf16[12,512,512]{2,1,0:T(8,128)(2,1)S(1)}) custom-call(bf16[1,256,512]{2,1,0:T(8,128)(2,1)} %hits_hbm.1, s32[2,1,256]{2,1,0:T(1,128)} %order_hbm.1, bf16[1,512,1536]{2,1,0:T(8,128)(2,1)} %w_qkv.1, bf16[1,512,512]{2,1,0:T(8,128)(2,1)} %w_out.1, bf16[1,512,2048]{2,1,0:T(8,128)(2,1)} %w_up.1, ...), custom_call_target="tpu_custom_call" | custom-call | flops 67108864 | bytes 13631488 | tf_op jit(solution)/shard_map/arrange/pallas_call | solution.py:67
  3.0 1.9 %collective-permute-start = (bf16[12,512,512]{2,1,0:T(8,128)(2,1)S(1)}, bf16[12,512,512]{2,1,0:T(8,128)(2,1)S(1)}, u32[]{:S(2)}, u32[]{:S(2)}) collective-permute-start(bf16[12,512,512]{2,1,0:T(8,128)(2,1)S(1)} %get-tuple-element.8.own), channel_id=1, source_target_pairs={{0,256},{256,0},{1,257},{257,1},{2,258},{258,2},{3,259},{259,3},{4... | collective-permute-start | bytes 18874376 | tf_op jit(solution)/shard_map/ppermute | solution.py:295
  5.0 0.0 copy-start
  5.0 0.0 copy-start.1
  5.0 6.7 %collective-permute-start.2 = (bf16[256,512]{1,0:T(8,128)(2,1)S(1)}, bf16[256,512]{1,0:T(8,128)(2,1)S(1)}, u32[]{:S(2)}, u32[]{:S(2)}) collective-permute-start(bf16[256,512]{1,0:T(8,128)(2,1)S(1)} %get-tuple-element.7.state), channel_id=1, source_target_pairs={{1,2},{2,1},{3,4},{4,3},{5,6},{6,5},{7,8},{8,7},{9,10},{10,9},{11,... | collective-permute-start | bytes 786440 | tf_op jit(solution)/shard_map/ppermute | solution.py:298
  11.6 1.9 %collective-permute-start.1 = (bf16[256,512]{1,0:T(8,128)(2,1)S(1)}, bf16[256,512]{1,0:T(8,128)(2,1)S(1)}, u32[]{:S(2)}, u32[]{:S(2)}) collective-permute-start(bf16[256,512]{1,0:T(8,128)(2,1)S(1)} %get-tuple-element.7.state), channel_id=1, source_target_pairs={{0,1},{1,0},{2,3},{3,2},{4,5},{5,4},{6,7},{7,6},{8,9},{9,8},{10,11... | collective-permute-start | bytes 786440 | tf_op jit(solution)/shard_map/ppermute | solution.py:299
  13.6 1.5 %collective-permute-done.came = bf16[12,512,512]{2,1,0:T(8,128)(2,1)S(1)} collective-permute-done((bf16[12,512,512]{2,1,0:T(8,128)(2,1)S(1)}, bf16[12,512,512]{2,1,0:T(8,128)(2,1)S(1)}, u32[]{:S(2)}, u32[]{:S(2)}) %collective-permute-start) | collective-permute-done | bytes 6291488 | tf_op jit(solution)/shard_map/ppermute | solution.py:295
  15.1 1.3 %project_0.1.mixed = bf16[256,1536]{1,0:T(8,128)(2,1)S(1)} custom-call(bf16[256,512]{1,0:T(8,128)(2,1)S(1)} %get-tuple-element.7.state, bf16[12,512,512]{2,1,0:T(8,128)(2,1)S(1)} %get-tuple-element.8.own, bf16[12,512,512]{2,1,0:T(8,128)(2,1)S(1)} %collective-permute-done.came), custom_call_target="tpu_custom_call" | custom-call | flops 402653184 | bytes 3145728 | tf_op jit(solution)/shard_map/project_0/pallas_call | solution.py:133
  16.4 4.6 %collective-permute-done.2.near_b = bf16[256,512]{1,0:T(8,128)(2,1)S(1)} collective-permute-done((bf16[256,512]{1,0:T(8,128)(2,1)S(1)}, bf16[256,512]{1,0:T(8,128)(2,1)S(1)}, u32[]{:S(2)}, u32[]{:S(2)}) %collective-permute-start.2) | collective-permute-done | bytes 262176 | tf_op jit(solution)/shard_map/ppermute | solution.py:298
  21.0 1.0 %collective-permute-done.1.near_a = bf16[256,512]{1,0:T(8,128)(2,1)S(1)} collective-permute-done((bf16[256,512]{1,0:T(8,128)(2,1)S(1)}, bf16[256,512]{1,0:T(8,128)(2,1)S(1)}, u32[]{:S(2)}, u32[]{:S(2)}) %collective-permute-start.1) | collective-permute-done | bytes 262176 | tf_op jit(solution)/shard_map/ppermute | solution.py:299
  22.0 0.0 copy-done
  22.0 0.0 copy-done.1
  22.0 6.8 %block_0.1.state = bf16[256,512]{1,0:T(8,128)(2,1)S(1)} custom-call(s32[2,2,3]{2,1,0:T(2,128)S(1)} %copy-done, s32[2,256]{1,0:T(2,128)S(1)} %copy-done.1, bf16[256,512]{1,0:T(8,128)(2,1)S(1)} %get-tuple-element.7.state, bf16[256,1536]{1,0:T(8,128)(2,1)S(1)} %project_0.1.mixed, bf16[256,512]{1,0:T(8,128)(2,1)S(1)} %collective-permute-done.1.near_a, ...), custom_call_target="tpu_custom_call" | custom-call | flops 4000000000 | bytes 8388608 | tf_op jit(solution)/shard_map/block_0/pallas_call | solution.py:268
  28.8 5.7 %collective-permute-start.4 = (bf16[256,512]{1,0:T(8,128)(2,1)S(1)}, bf16[256,512]{1,0:T(8,128)(2,1)S(1)}, u32[]{:S(2)}, u32[]{:S(2)}) collective-permute-start(bf16[256,512]{1,0:T(8,128)(2,1)S(1)} %block_0.1.state), channel_id=1, source_target_pairs={{1,2},{2,1},{3,4},{4,3},{5,6},{6,5},{7,8},{8,7},{9,10},{10,9},{11,... | collective-permute-start | bytes 786440 | tf_op jit(solution)/shard_map/ppermute | solution.py:298
  34.5 1.9 %collective-permute-start.3 = (bf16[256,512]{1,0:T(8,128)(2,1)S(1)}, bf16[256,512]{1,0:T(8,128)(2,1)S(1)}, u32[]{:S(2)}, u32[]{:S(2)}) collective-permute-start(bf16[256,512]{1,0:T(8,128)(2,1)S(1)} %block_0.1.state), channel_id=1, source_target_pairs={{0,1},{1,0},{2,3},{3,2},{4,5},{5,4},{6,7},{7,6},{8,9},{9,8},{10,11... | collective-permute-start | bytes 786440 | tf_op jit(solution)/shard_map/ppermute | solution.py:299
  36.4 1.3 %project_1.1.mixed = bf16[256,1536]{1,0:T(8,128)(2,1)S(1)} custom-call(bf16[256,512]{1,0:T(8,128)(2,1)S(1)} %block_0.1.state, bf16[12,512,512]{2,1,0:T(8,128)(2,1)S(1)} %get-tuple-element.8.own, bf16[12,512,512]{2,1,0:T(8,128)(2,1)S(1)} %collective-permute-done.came), custom_call_target="tpu_custom_call" | custom-call | flops 402653184 | bytes 3145728 | tf_op jit(solution)/shard_map/project_1/pallas_call | solution.py:133
  37.7 5.9 %collective-permute-done.4.near_b = bf16[256,512]{1,0:T(8,128)(2,1)S(1)} collective-permute-done((bf16[256,512]{1,0:T(8,128)(2,1)S(1)}, bf16[256,512]{1,0:T(8,128)(2,1)S(1)}, u32[]{:S(2)}, u32[]{:S(2)}) %collective-permute-start.4) | collective-permute-done | bytes 262176 | tf_op jit(solution)/shard_map/ppermute | solution.py:298
  43.7 0.3 collective-permute-done.3.near_a
  44.0 7.7 %block_1.1 = bf16[256,512]{1,0:T(8,128)(2,1)} custom-call(s32[2,2,3]{2,1,0:T(2,128)S(1)} %copy-done, s32[2,256]{1,0:T(2,128)S(1)} %copy-done.1, bf16[256,512]{1,0:T(8,128)(2,1)S(1)} %block_0.1.state, bf16[256,1536]{1,0:T(8,128)(2,1)S(1)} %project_1.1.mixed, bf16[256,512]{1,0:T(8,128)(2,1)S(1)} %collective-permute-done.3.near_a, ...), custom_call_target="tpu_custom_call" | custom-call | flops 4000000000 | bytes 8388608 | tf_op jit(solution)/shard_map/block_1/pallas_call | solution.py:268
Async XLA Ops:
  3.0 12.1 %collective-permute-start = (bf16[12,512,512]{2,1,0:T(8,128)(2,1)S(1)}, bf16[12,512,512]{2,1,0:T(8,128)(2,1)S(1)}, u32[]{:S(2)}, u32[]{:S(2)}) collective-permute-start(bf16[12,512,512]{2,1,0:T(8,128)(2,1)S(1)} %get-tuple-element.8.own), channel_id=1, source_target_pairs={{0,256},{256,0},{1,257},{257,1},{2,258},{258,2},{3,259},{259,3},{4... | collective-permute-start | bytes 18874376 | tf_op jit(solution)/shard_map/ppermute | solution.py:295
  5.0 17.0 %copy-start = (s32[2,2,3]{2,1,0:T(2,128)S(1)}, s32[2,2,3]{2,1,0:T(2,128)}, u32[]{:S(2)}) copy-start(s32[2,2,3]{2,1,0:T(2,128)} %links.3) | copy-start | bytes 148
  5.0 17.0 %copy-start.1 = (s32[2,256]{1,0:T(2,128)S(1)}, s32[2,256]{1,0:T(2,128)}, u32[]{:S(2)}) copy-start(s32[2,256]{1,0:T(2,128)} %counts.3) | copy-start | bytes 6148
  5.0 16.0 %collective-permute-start.2 = (bf16[256,512]{1,0:T(8,128)(2,1)S(1)}, bf16[256,512]{1,0:T(8,128)(2,1)S(1)}, u32[]{:S(2)}, u32[]{:S(2)}) collective-permute-start(bf16[256,512]{1,0:T(8,128)(2,1)S(1)} %get-tuple-element.7.state), channel_id=1, source_target_pairs={{1,2},{2,1},{3,4},{4,3},{5,6},{6,5},{7,8},{8,7},{9,10},{10,9},{11,... | collective-permute-start | bytes 786440 | tf_op jit(solution)/shard_map/ppermute | solution.py:298
  11.6 10.3 %collective-permute-start.1 = (bf16[256,512]{1,0:T(8,128)(2,1)S(1)}, bf16[256,512]{1,0:T(8,128)(2,1)S(1)}, u32[]{:S(2)}, u32[]{:S(2)}) collective-permute-start(bf16[256,512]{1,0:T(8,128)(2,1)S(1)} %get-tuple-element.7.state), channel_id=1, source_target_pairs={{0,1},{1,0},{2,3},{3,2},{4,5},{5,4},{6,7},{7,6},{8,9},{9,8},{10,11... | collective-permute-start | bytes 786440 | tf_op jit(solution)/shard_map/ppermute | solution.py:299
  28.8 14.9 %collective-permute-start.4 = (bf16[256,512]{1,0:T(8,128)(2,1)S(1)}, bf16[256,512]{1,0:T(8,128)(2,1)S(1)}, u32[]{:S(2)}, u32[]{:S(2)}) collective-permute-start(bf16[256,512]{1,0:T(8,128)(2,1)S(1)} %block_0.1.state), channel_id=1, source_target_pairs={{1,2},{2,1},{3,4},{4,3},{5,6},{6,5},{7,8},{8,7},{9,10},{10,9},{11,... | collective-permute-start | bytes 786440 | tf_op jit(solution)/shard_map/ppermute | solution.py:298
  34.5 9.5 %collective-permute-start.3 = (bf16[256,512]{1,0:T(8,128)(2,1)S(1)}, bf16[256,512]{1,0:T(8,128)(2,1)S(1)}, u32[]{:S(2)}, u32[]{:S(2)}) collective-permute-start(bf16[256,512]{1,0:T(8,128)(2,1)S(1)} %block_0.1.state), channel_id=1, source_target_pairs={{0,1},{1,0},{2,3},{3,2},{4,5},{5,4},{6,7},{7,6},{8,9},{9,8},{10,11... | collective-permute-start | bytes 786440 | tf_op jit(solution)/shard_map/ppermute | solution.py:299

commit v2 on v1

v2 whole, which is shorter than its diff:
```python
import functools

import jax
import jax.numpy as jnp
from jax import lax
from jax.experimental import pallas as pl
from jax.experimental.pallas import tpu as pltpu
from jax.sharding import PartitionSpec as P


HEADS = 8
HEAD = 64
D = 512
PATCH = 128
LINKS = 3
PAIRS = HEADS // 2
EPS = 1e-05
FF = 2048
WIDTH = 1024
LIMIT = 16 << 20
BF16 = jnp.bfloat16
F32 = jnp.float32

QKV, OUT, FIRST = 0, 3, 4


def dot(a, b):
    return jnp.dot(a, b, preferred_element_type=F32)


def normalize(values):
    center = jnp.mean(values, axis=-1, keepdims=True)
    shifted = values - center
    spread = jnp.mean(shifted * shifted, axis=-1, keepdims=True)
    return (shifted * lax.rsqrt(spread + EPS)).astype(BF16)


def gelu(x):
    return 0.5 * x * (1.0 + lax.erf(x * (0.5**0.5)))


def copies_of(pairs, sem):
    return [pltpu.make_async_copy(a, b, sem.at[i]) for i, (a, b) in enumerate(pairs)]


def arrange_kernel(hits_hbm, order_hbm, w_qkv, w_out, ordered, packed, hits, order, sem):
    event = lax.axis_index("section")
    pairs = [(hits_hbm.at[0], hits), (order_hbm.at[event], order)]
    for i in range(3):
        pairs.append((w_qkv.at[0, :, pl.ds(i * D, D)], packed.at[QKV + i]))
    pairs.append((w_out.at[0], packed.at[OUT]))
    copies = copies_of(pairs, sem)
    for copy in copies:
        copy.start()
    copies[0].wait()
    copies[1].wait()
    rows = hits.shape[0]
    source_row = lax.broadcasted_iota(jnp.int32, (rows, rows), 0)
    chosen = jnp.where(source_row == order[...], 1.0, 0.0).T.astype(BF16)
    ordered[...] = dot(chosen, hits[...]).astype(BF16)
    for copy in copies[2:]:
        copy.wait()


def arrange(hits, order, w_qkv, w_out):
    rows = hits.shape[1]
    vmem = pl.BlockSpec(memory_space=pltpu.VMEM)
    args = [pltpu.with_memory_space_constraint(a, pltpu.HBM) for a in (hits, order, w_qkv, w_out)]
    return pl.pallas_call(
        arrange_kernel,
        name="arrange",
        out_shape=(
            jax.ShapeDtypeStruct((rows, D), BF16),
            jax.ShapeDtypeStruct((FIRST, D, D), BF16),
        ),
        in_specs=[pl.BlockSpec(memory_space=pltpu.HBM)] * 4,
        out_specs=(vmem, vmem),
        scratch_shapes=[
            pltpu.VMEM((rows, D), BF16),
            pltpu.VMEM((1, rows), jnp.int32),
            pltpu.SemaphoreType.DMA((FIRST + 2,)),
        ],
        compiler_params=pltpu.CompilerParams(vmem_limit_bytes=20 << 20),
        cost_estimate=pl.CostEstimate(
            flops=2 * rows * rows * D, bytes_accessed=4 << 20, transcendentals=0
        ),
    )(*args)


def with_weights(block, own, came, body):
    section = lax.axis_index("section")

    @pl.when(section == block)
    def _():
        body(*own)

    @pl.when(section != block)
    def _():
        body(*came)


def prepare_kernel(block, state, own, came, queries, mixed):
    low = lax.broadcasted_iota(jnp.int32, (PATCH, 128), 1) < HEAD
    scale = jnp.asarray(HEAD**-0.5, BF16)
    low_scale = jnp.where(low, scale, 0.0).astype(BF16)
    high_scale = jnp.where(low, 0.0, scale).astype(BF16)

    def body(weights):
        normed = normalize(state[...].astype(F32))
        query = dot(normed, weights[QKV]).astype(BF16)
        for patch in range(state.shape[0] // PATCH):
            for pair in range(PAIRS):
                part = query[patch * PATCH : (patch + 1) * PATCH, pair * 128 : (pair + 1) * 128]
                queries[patch, pair, 0:PATCH, :] = part * low_scale
                queries[patch, pair, PATCH : 2 * PATCH, :] = part * high_scale
        mixed[:, 0:D] = dot(normed, weights[QKV + 1]).astype(BF16)
        mixed[:, D : 2 * D] = dot(normed, weights[QKV + 2]).astype(BF16)

    with_weights(block, (own,), (came,), body)


def prepare(block, state, own, came):
    rows = state.shape[0]
    vmem = pl.BlockSpec(memory_space=pltpu.VMEM)
    return pl.pallas_call(
        functools.partial(prepare_kernel, block),
        out_shape=(
            jax.ShapeDtypeStruct((rows // PATCH, PAIRS, 2 * PATCH, 128), BF16),
            jax.ShapeDtypeStruct((rows, 2 * D), BF16),
        ),
        in_specs=[vmem] * 3,
        out_specs=(vmem, vmem),
        compiler_params=pltpu.CompilerParams(vmem_limit_bytes=LIMIT),
        cost_estimate=pl.CostEstimate(
            flops=6 * rows * D * D, bytes_accessed=4 << 20, transcendentals=0
        ),
    )(state, own, came)


def attend_kernel(
    block,
    links,
    counts,
    state,
    queries,
    mixed,
    near_a,
    near_b,
    own,
    came,
    middle,
    near,
    attended,
    sem,
):
    event = lax.axis_index("section")
    region = lax.axis_index("region")
    regions = counts.shape[1]
    rows = state.shape[0]
    patches = rows // PATCH
    bring = pltpu.make_async_copy(mixed, near.at[pl.ds(0, rows)], sem)
    bring.start()
    even = lax.rem(region, 2) == 0
    region_a = jnp.where(even, region + 1, region - 1)
    region_b = jnp.where(even, region - 1, region + 1)
    count_own = counts[event, region]
    count_a = counts[event, jnp.clip(region_a, 0, regions - 1)]
    count_b = counts[event, jnp.clip(region_b, 0, regions - 1)]
    key_lane = lax.broadcasted_iota(jnp.int32, (2 * PATCH, PATCH), 1)
    low = lax.broadcasted_iota(jnp.int32, (PATCH, 128), 1) < HEAD
    ones = jnp.ones((PATCH, 128), BF16)

    def body(weights):
        for i, other in enumerate((near_a, near_b)):
            normed = normalize(other[...].astype(F32))
            here = slice((i + 1) * rows, (i + 2) * rows)
            near[here, 0:D] = dot(normed, weights[QKV + 1]).astype(BF16)
            near[here, D : 2 * D] = dot(normed, weights[QKV + 2]).astype(BF16)
        bring.wait()
        for patch in range(patches):
            places, valid = [], []
            for link in range(LINKS):
                linked = links[event, patch, link]
                owner = lax.div(linked, patches)
                half = lax.rem(linked, patches)
                base = jnp.where(owner == region, 0, jnp.where(owner == region_a, 1, 2))
                count = jnp.where(base == 0, count_own, jnp.where(base == 1, count_a, count_b))
                places.append(pl.multiple_of((base * patches + half) * PATCH, PATCH))
                valid.append(key_lane < count - half * PATCH)
            for pair in range(PAIRS):
                across = slice(pair * 128, (pair + 1) * 128)
                query = queries[patch, pair]
                scores = []
                for link in range(LINKS):
                    score = lax.dot_general(
                        query,
                        near[pl.ds(places[link], PATCH), across],
                        (((1,), (1,)), ((), ())),
                        preferred_element_type=F32,
                    )
                    scores.append(jnp.where(valid[link], score, -1e30))
                top = jnp.max(functools.reduce(jnp.maximum, scores), axis=-1, keepdims=True)
                total = None
                for link in range(LINKS):
                    weighed = jnp.exp(scores[link] - top).astype(BF16)
                    value = near[pl.ds(places[link], PATCH), D + pair * 128 : D + (pair + 1) * 128]
                    part = dot(weighed, jnp.concatenate([value, ones], axis=1))
                    total = part if total is None else total + part
                summed = jnp.where(low, total[:PATCH, :128], total[PATCH:, :128])
                mass = jnp.where(low, total[:PATCH, 128:], total[PATCH:, 128:])
                attended[patch * PATCH : (patch + 1) * PATCH, across] = (summed / mass).astype(BF16)
        middle[...] = (state[...].astype(F32) + dot(attended[...], weights[OUT])).astype(BF16)

    with_weights(block, (own,), (came,), body)


def attend(block, links, counts, state, queries, mixed, near_a, near_b, own, came):
    rows = state.shape[0]
    vmem = pl.BlockSpec(memory_space=pltpu.VMEM)
    smem = pl.BlockSpec(memory_space=pltpu.SMEM)
    return pl.pallas_call(
        functools.partial(attend_kernel, block),
        out_shape=jax.ShapeDtypeStruct((rows, D), BF16),
        in_specs=[smem, smem] + [vmem] * 7,
        out_specs=vmem,
        scratch_shapes=[
            pltpu.VMEM((3 * rows, 2 * D), BF16),
            pltpu.VMEM((rows, D), BF16),
            pltpu.SemaphoreType.DMA,
        ],
        compiler_params=pltpu.CompilerParams(vmem_limit_bytes=LIMIT),
        cost_estimate=pl.CostEstimate(
            flops=10**9, bytes_accessed=4 << 20, transcendentals=8 * 10**5
        ),
    )(links, counts, state, queries, mixed, near_a, near_b, own, came)


def feed_kernel(block, last, counts, middle_ref, up_own, down_own, up_came, down_came, result):
    def body(up, down):
        middle = middle_ref[...].astype(F32)
        normed = normalize(middle)
        total = middle
        for part in range(0, FF, WIDTH):
            hidden = gelu(dot(normed, up[0, :, part : part + WIDTH])).astype(BF16)
            total = total + dot(hidden, down[0, part : part + WIDTH, :])
        total = total.astype(BF16)
        if last:
            count = counts[lax.axis_index("section"), lax.axis_index("region")]
            row = lax.broadcasted_iota(jnp.int32, total.shape, 0)
            total = jnp.where(row < count, total.astype(F32), 0.0).astype(BF16)
        result[...] = total

    with_weights(block, (up_own, down_own), (up_came, down_came), body)


def feed(block, last, counts, middle, *weights):
    rows = middle.shape[0]
    vmem = pl.BlockSpec(memory_space=pltpu.VMEM)
    smem = pl.BlockSpec(memory_space=pltpu.SMEM)
    return pl.pallas_call(
        functools.partial(feed_kernel, block, last),
        out_shape=jax.ShapeDtypeStruct((rows, D), BF16),
        in_specs=[smem] + [vmem] * 5,
        out_specs=vmem,
        compiler_params=pltpu.CompilerParams(vmem_limit_bytes=LIMIT),
        cost_estimate=pl.CostEstimate(
            flops=4 * rows * FF * D, bytes_accessed=5 << 20, transcendentals=10**6
        ),
    )(counts, middle, *weights)


def per_device(hits, order, links, counts, w_qkv, w_out, w_up, w_down):
    regions = counts.shape[1]
    pairs_a = [(i, i ^ 1) for i in range(regions)]
    pairs_b = []
    for i in range(1, regions - 1, 2):
        pairs_b += [(i, i + 1), (i + 1, i)]
    swap = [(0, 1), (1, 0)]
    ordered, own = arrange(hits, order, w_qkv, w_out)
    state = ordered
    for block in range(2):
        near_b = lax.ppermute(state, "region", pairs_b)
        if block == 0:
            came = lax.ppermute(own, "section", swap)
        near_a = lax.ppermute(state, "region", pairs_a)
        if block == 0:
            up_came = lax.ppermute(w_up, "section", swap)
            down_came = lax.ppermute(w_down, "section", swap)
            second = (w_up, w_down, up_came, down_came)
        queries, mixed = prepare(block, state, own, came)
        middle = attend(block, links, counts, state, queries, mixed, near_a, near_b, own, came)
        state = feed(block, block == 1, counts, middle, *second)
    return state[None]


def solution(mesh):
    in_specs = (
        P("section", "region", None),
        P(None, "region", None),
        P(None, "region", None),
        P(),
        P("section", None, None),
        P("section", None, None),
        P("section", None, None),
        P("section", None, None),
    )
    out_specs = P("section", "region", None)
    return jax.shard_map(
        per_device, mesh=mesh, in_specs=in_specs, out_specs=out_specs, check_vma=False
    )
```

time: 52 us -> 54.1 us (1.040)
  starting transfers between devices: 18.1 us -> 22.5 us
  Pallas kernels: 20.1 us -> 16.8 us
  waiting for transfers between devices: 13.3 us -> 14.3 us
    ppermute x1 -> x3, starting transfers between devices: 1.92 us -> 6.25 us  [the longest x1 2.41 us: per_device(): up_came = lax.ppermute(w_up, 'section', swap)]
    ppermute x2, waiting for transfers between devices: 10.6 us -> 13.1 us  [per_device(): near_b = lax.ppermute(state, 'region', pairs_b)]
    pallas_call x4 -> x6, Pallas kernels: 17.1 us -> 15 us  [the longest x2 8.43 us: attend(): pl.pallas_call(functools.partial(attend_kernel, block), out_shape=jax.Sha...]
    ppermute x1 -> x3, waiting for transfers between devices: 1.5 us -> 0.01 us  [the longest x1 0.01 us: per_device(): up_came = lax.ppermute(w_up, 'section', swap)]
    pallas_call x1, Pallas kernels: 3.02 us -> 1.82 us  [arrange(): pl.pallas_call(arrange_kernel, name='arrange', out_shape=(jax.ShapeDtypeS...]
  transfers between devices with their start and end apart: 5 -> 7, of which waited for: 5 -> 4; matrix products, arithmetic and copies ran while one was open for 0% -> 0% of each run, Pallas kernels for 5% -> 11%
where the time goes in v2:
time: 54.1 us; the launch traced here: 53.8 us
  starting transfers between devices  22.5 us (42%)
  Pallas kernels  16.8 us (31%)
  waiting for transfers between devices  14.3 us (26%)
    ppermute x2, waiting for transfers between devices, per_device(): near_b = lax.ppermute(state, 'region', pairs_b)  13.1 us
    ppermute x2, starting transfers between devices, per_device(): near_b = lax.ppermute(state, 'region', pairs_b)  12.4 us
    pallas_call x2, Pallas kernels, attend(): pl.pallas_call(functools.partial(attend_kernel, block), out_shape=jax.Sha...  8.43 us
    pallas_call x2, Pallas kernels, feed(): pl.pallas_call(functools.partial(feed_kernel, block, last), out_shape=jax...  4.99 us
    ppermute x2, starting transfers between devices, per_device(): near_a = lax.ppermute(state, 'region', pairs_a)  3.84 us
    ppermute x1, starting transfers between devices, per_device(): up_came = lax.ppermute(w_up, 'section', swap)  2.41 us
    ppermute x1, starting transfers between devices, per_device(): down_came = lax.ppermute(w_down, 'section', swap)  1.92 us
    ppermute x1, starting transfers between devices, per_device(): came = lax.ppermute(own, 'section', swap)  1.92 us
  transfers between devices with their start and end apart: 7, of which 4 were waited for; matrix products, arithmetic and copies ran while one was open for 0% of the time, Pallas kernels for 11%

profile of v2, /device:TPU:256, one launch (start us, length us, event | category | flops | bytes accessed | tf_op | source)
XLA Modules:
  0.0 53.8 jit_solution(11722474259868882231)
XLA Ops:
  0.0 0.0 copy-start
  0.0 1.8 %arrange.1 = (bf16[256,512]{1,0:T(8,128)(2,1)S(1)}, bf16[4,512,512]{2,1,0:T(8,128)(2,1)S(1)}) custom-call(bf16[1,256,512]{2,1,0:T(8,128)(2,1)} %hits_hbm.1, s32[2,1,256]{2,1,0:T(1,128)} %order_hbm.1, bf16[1,512,1536]{2,1,0:T(8,128)(2,1)} %w_qkv.1, bf16[1,512,512]{2,1,0:T(8,128)(2,1)} %w_out.1), custom_call_target="tpu_custom_call" | custom-call | flops 67108864 | bytes 4194304 | tf_op jit(solution)/shard_map/arrange/pallas_call | solution.py:69
  1.8 1.9 %collective-permute-start = (bf16[4,512,512]{2,1,0:T(8,128)(2,1)S(1)}, bf16[4,512,512]{2,1,0:T(8,128)(2,1)S(1)}, u32[]{:S(2)}, u32[]{:S(2)}) collective-permute-start(bf16[4,512,512]{2,1,0:T(8,128)(2,1)S(1)} %get-tuple-element.12.own), channel_id=1, source_target_pairs={{0,256},{256,0},{1,257},{257,1},{2,258},{258,2},{3,259},{259,3},{4... | collective-permute-start | bytes 6291464 | tf_op jit(solution)/shard_map/ppermute | solution.py:284
  3.8 0.0 copy-done
  3.8 2.4 %collective-permute-start.3 = (bf16[1,512,2048]{2,1,0:T(8,128)(2,1)S(1)}, bf16[1,512,2048]{2,1,0:T(8,128)(2,1)S(1)}, u32[]{:S(2)}, u32[]{:S(2)}) collective-permute-start(bf16[1,512,2048]{2,1,0:T(8,128)(2,1)S(1)} %copy-done), channel_id=1, source_target_pairs={{0,256},{256,0},{1,257},{257,1},{2,258},{258,2},{3,259},{259,3},{4... | collective-permute-start | bytes 6291464 | tf_op jit(solution)/shard_map/ppermute | solution.py:287
  6.2 1.9 %collective-permute-start.4 = (bf16[1,2048,512]{2,1,0:T(8,128)(2,1)}, bf16[1,2048,512]{2,1,0:T(8,128)(2,1)S(1)}, u32[]{:S(2)}, u32[]{:S(2)}) collective-permute-start(bf16[1,2048,512]{2,1,0:T(8,128)(2,1)} %down_own.3), channel_id=1, source_target_pairs={{0,256},{256,0},{1,257},{257,1},{2,258},{258,2},{3,259},{259,3},{4... | collective-permute-start | bytes 6291464 | tf_op jit(solution)/shard_map/ppermute | solution.py:288
  8.1 0.0 copy-start.2
  8.1 0.0 copy-start.3
  8.1 6.7 %collective-permute-start.2 = (bf16[256,512]{1,0:T(8,128)(2,1)S(1)}, bf16[256,512]{1,0:T(8,128)(2,1)S(1)}, u32[]{:S(2)}, u32[]{:S(2)}) collective-permute-start(bf16[256,512]{1,0:T(8,128)(2,1)S(1)} %get-tuple-element.11.state), channel_id=1, source_target_pairs={{1,2},{2,1},{3,4},{4,3},{5,6},{6,5},{7,8},{8,7},{9,10},{10,9},{11,... | collective-permute-start | bytes 786440 | tf_op jit(solution)/shard_map/ppermute | solution.py:282
  14.8 1.9 %collective-permute-start.1 = (bf16[256,512]{1,0:T(8,128)(2,1)S(1)}, bf16[256,512]{1,0:T(8,128)(2,1)S(1)}, u32[]{:S(2)}, u32[]{:S(2)}) collective-permute-start(bf16[256,512]{1,0:T(8,128)(2,1)S(1)} %get-tuple-element.11.state), channel_id=1, source_target_pairs={{0,1},{1,0},{2,3},{3,2},{4,5},{5,4},{6,7},{7,6},{8,9},{9,8},{10,11... | collective-permute-start | bytes 786440 | tf_op jit(solution)/shard_map/ppermute | solution.py:285
  16.7 0.0 collective-permute-done.came
  16.7 0.8 %shard_map.82 = (bf16[2,4,256,128]{3,2,1,0:T(8,128)(2,1)S(1)}, bf16[256,1024]{1,0:T(8,128)(2,1)S(1)}) custom-call(bf16[256,512]{1,0:T(8,128)(2,1)S(1)} %get-tuple-element.11.state, bf16[4,512,512]{2,1,0:T(8,128)(2,1)S(1)} %get-tuple-element.12.own, bf16[4,512,512]{2,1,0:T(8,128)(2,1)S(1)} %collective-permute-done.came), custom_call_target="tpu_custom_call" | custom-call | flops 402653184 | bytes 4194304 | tf_op jit(solution)/shard_map/pallas_call | solution.py:125
  17.5 6.6 %collective-permute-done.2.near_b = bf16[256,512]{1,0:T(8,128)(2,1)S(1)} collective-permute-done((bf16[256,512]{1,0:T(8,128)(2,1)S(1)}, bf16[256,512]{1,0:T(8,128)(2,1)S(1)}, u32[]{:S(2)}, u32[]{:S(2)}) %collective-permute-start.2) | collective-permute-done | bytes 262176 | tf_op jit(solution)/shard_map/ppermute | solution.py:282
  24.2 1.0 %collective-permute-done.1.near_a = bf16[256,512]{1,0:T(8,128)(2,1)S(1)} collective-permute-done((bf16[256,512]{1,0:T(8,128)(2,1)S(1)}, bf16[256,512]{1,0:T(8,128)(2,1)S(1)}, u32[]{:S(2)}, u32[]{:S(2)}) %collective-permute-start.1) | collective-permute-done | bytes 262176 | tf_op jit(solution)/shard_map/ppermute | solution.py:285
  25.1 0.0 copy-done.2
  25.1 0.0 copy-done.3
  25.1 0.0 copy-start.1
  25.1 4.1 %shard_map.83.middle_ref = bf16[256,512]{1,0:T(8,128)(2,1)S(1)} custom-call(s32[2,2,3]{2,1,0:T(2,128)S(1)} %copy-done.3, s32[2,256]{1,0:T(2,128)S(1)} %copy-done.2, bf16[256,512]{1,0:T(8,128)(2,1)S(1)} %get-tuple-element.11.state, bf16[2,4,256,128]{3,2,1,0:T(8,128)(2,1)S(1)} %get-tuple-element.13.queries, bf16[256,1024]{1,0:T(8,128)(2,1)S(1)} %get-tuple-element.14.mixed, ...), custom_call_target="tpu_custom_call" | custom-call | flops 1000000000 | bytes 4194304 | tf_op jit(solution)/shard_map/pallas_call | solution.py:221
  29.3 0.0 collective-permute-done.3.up_came
  29.3 0.0 collective-permute-done.4.down_came
  29.3 0.0 copy-done.1
  29.3 2.1 %shard_map.84.state = bf16[256,512]{1,0:T(8,128)(2,1)S(1)} custom-call(s32[2,256]{1,0:T(2,128)S(1)} %copy-done.2, bf16[256,512]{1,0:T(8,128)(2,1)S(1)} %shard_map.83.middle_ref, bf16[1,512,2048]{2,1,0:T(8,128)(2,1)S(1)} %copy-done, bf16[1,2048,512]{2,1,0:T(8,128)(2,1)S(1)} %copy-done.1, bf16[1,512,2048]{2,1,0:T(8,128)(2,1)S(1)} %collective-permute-done.3.up_came, ...), custom_call_target="tpu_custom_call" | custom-call | flops 1073741824 | bytes 5242880 | tf_op jit(solution)/shard_map/pallas_call | solution.py:260
  31.4 5.7 %collective-permute-start.6 = (bf16[256,512]{1,0:T(8,128)(2,1)S(1)}, bf16[256,512]{1,0:T(8,128)(2,1)S(1)}, u32[]{:S(2)}, u32[]{:S(2)}) collective-permute-start(bf16[256,512]{1,0:T(8,128)(2,1)S(1)} %shard_map.84.state), channel_id=1, source_target_pairs={{1,2},{2,1},{3,4},{4,3},{5,6},{6,5},{7,8},{8,7},{9,10},{10,9},{11,... | collective-permute-start | bytes 786440 | tf_op jit(solution)/shard_map/ppermute | solution.py:282
  37.2 1.9 %collective-permute-start.5 = (bf16[256,512]{1,0:T(8,128)(2,1)S(1)}, bf16[256,512]{1,0:T(8,128)(2,1)S(1)}, u32[]{:S(2)}, u32[]{:S(2)}) collective-permute-start(bf16[256,512]{1,0:T(8,128)(2,1)S(1)} %shard_map.84.state), channel_id=1, source_target_pairs={{0,1},{1,0},{2,3},{3,2},{4,5},{5,4},{6,7},{7,6},{8,9},{9,8},{10,11... | collective-permute-start | bytes 786440 | tf_op jit(solution)/shard_map/ppermute | solution.py:285
  39.1 0.8 %shard_map.85 = (bf16[2,4,256,128]{3,2,1,0:T(8,128)(2,1)S(1)}, bf16[256,1024]{1,0:T(8,128)(2,1)S(1)}) custom-call(bf16[256,512]{1,0:T(8,128)(2,1)S(1)} %shard_map.84.state, bf16[4,512,512]{2,1,0:T(8,128)(2,1)S(1)} %get-tuple-element.12.own, bf16[4,512,512]{2,1,0:T(8,128)(2,1)S(1)} %collective-permute-done.came), custom_call_target="tpu_custom_call" | custom-call | flops 402653184 | bytes 4194304 | tf_op jit(solution)/shard_map/pallas_call | solution.py:125
  39.9 6.5 %collective-permute-done.6.near_b = bf16[256,512]{1,0:T(8,128)(2,1)S(1)} collective-permute-done((bf16[256,512]{1,0:T(8,128)(2,1)S(1)}, bf16[256,512]{1,0:T(8,128)(2,1)S(1)}, u32[]{:S(2)}, u32[]{:S(2)}) %collective-permute-start.6) | collective-permute-done | bytes 262176 | tf_op jit(solution)/shard_map/ppermute | solution.py:282
  46.3 0.3 collective-permute-done.5.near_a
  46.6 4.3 %shard_map.86.middle_ref = bf16[256,512]{1,0:T(8,128)(2,1)S(1)} custom-call(s32[2,2,3]{2,1,0:T(2,128)S(1)} %copy-done.3, s32[2,256]{1,0:T(2,128)S(1)} %copy-done.2, bf16[256,512]{1,0:T(8,128)(2,1)S(1)} %shard_map.84.state, bf16[2,4,256,128]{3,2,1,0:T(8,128)(2,1)S(1)} %get-tuple-element.15.queries, bf16[256,1024]{1,0:T(8,128)(2,1)S(1)} %get-tuple-element.16.mixed, ...), custom_call_target="tpu_custom_call" | custom-call | flops 1000000000 | bytes 4194304 | tf_op jit(solution)/shard_map/pallas_call | solution.py:221
  50.9 2.9 %shard_map.87 = bf16[256,512]{1,0:T(8,128)(2,1)} custom-call(s32[2,256]{1,0:T(2,128)S(1)} %copy-done.2, bf16[256,512]{1,0:T(8,128)(2,1)S(1)} %shard_map.86.middle_ref, bf16[1,512,2048]{2,1,0:T(8,128)(2,1)S(1)} %copy-done, bf16[1,2048,512]{2,1,0:T(8,128)(2,1)S(1)} %copy-done.1, bf16[1,512,2048]{2,1,0:T(8,128)(2,1)S(1)} %collective-permute-done.3.up_came, ...), custom_call_target="tpu_custom_call" | custom-call | flops 1073741824 | bytes 5242880 | tf_op jit(solution)/shard_map/pallas_call | solution.py:260
Async XLA Ops:
  0.0 3.8 %copy-start = (bf16[1,512,2048]{2,1,0:T(8,128)(2,1)S(1)}, bf16[1,512,2048]{2,1,0:T(8,128)(2,1)}, u32[]{:S(2)}) copy-start(bf16[1,512,2048]{2,1,0:T(8,128)(2,1)} %up_own.3) | copy-start | bytes 6291460
  1.8 14.9 %collective-permute-start = (bf16[4,512,512]{2,1,0:T(8,128)(2,1)S(1)}, bf16[4,512,512]{2,1,0:T(8,128)(2,1)S(1)}, u32[]{:S(2)}, u32[]{:S(2)}) collective-permute-start(bf16[4,512,512]{2,1,0:T(8,128)(2,1)S(1)} %get-tuple-element.12.own), channel_id=1, source_target_pairs={{0,256},{256,0},{1,257},{257,1},{2,258},{258,2},{3,259},{259,3},{4... | collective-permute-start | bytes 6291464 | tf_op jit(solution)/shard_map/ppermute | solution.py:284
  3.8 25.5 %collective-permute-start.3 = (bf16[1,512,2048]{2,1,0:T(8,128)(2,1)S(1)}, bf16[1,512,2048]{2,1,0:T(8,128)(2,1)S(1)}, u32[]{:S(2)}, u32[]{:S(2)}) collective-permute-start(bf16[1,512,2048]{2,1,0:T(8,128)(2,1)S(1)} %copy-done), channel_id=1, source_target_pairs={{0,256},{256,0},{1,257},{257,1},{2,258},{258,2},{3,259},{259,3},{4... | collective-permute-start | bytes 6291464 | tf_op jit(solution)/shard_map/ppermute | solution.py:287
  6.2 23.1 %collective-permute-start.4 = (bf16[1,2048,512]{2,1,0:T(8,128)(2,1)}, bf16[1,2048,512]{2,1,0:T(8,128)(2,1)S(1)}, u32[]{:S(2)}, u32[]{:S(2)}) collective-permute-start(bf16[1,2048,512]{2,1,0:T(8,128)(2,1)} %down_own.3), channel_id=1, source_target_pairs={{0,256},{256,0},{1,257},{257,1},{2,258},{258,2},{3,259},{259,3},{4... | collective-permute-start | bytes 6291464 | tf_op jit(solution)/shard_map/ppermute | solution.py:288
  8.1 17.0 %copy-start.2 = (s32[2,256]{1,0:T(2,128)S(1)}, s32[2,256]{1,0:T(2,128)}, u32[]{:S(2)}) copy-start(s32[2,256]{1,0:T(2,128)} %counts.7) | copy-start | bytes 6148
  8.1 17.0 %copy-start.3 = (s32[2,2,3]{2,1,0:T(2,128)S(1)}, s32[2,2,3]{2,1,0:T(2,128)}, u32[]{:S(2)}) copy-start(s32[2,2,3]{2,1,0:T(2,128)} %links.3) | copy-start | bytes 148
  8.1 16.0 %collective-permute-start.2 = (bf16[256,512]{1,0:T(8,128)(2,1)S(1)}, bf16[256,512]{1,0:T(8,128)(2,1)S(1)}, u32[]{:S(2)}, u32[]{:S(2)}) collective-permute-start(bf16[256,512]{1,0:T(8,128)(2,1)S(1)} %get-tuple-element.11.state), channel_id=1, source_target_pairs={{1,2},{2,1},{3,4},{4,3},{5,6},{6,5},{7,8},{8,7},{9,10},{10,9},{11,... | collective-permute-start | bytes 786440 | tf_op jit(solution)/shard_map/ppermute | solution.py:282
  14.8 10.3 %collective-permute-start.1 = (bf16[256,512]{1,0:T(8,128)(2,1)S(1)}, bf16[256,512]{1,0:T(8,128)(2,1)S(1)}, u32[]{:S(2)}, u32[]{:S(2)}) collective-permute-start(bf16[256,512]{1,0:T(8,128)(2,1)S(1)} %get-tuple-element.11.state), channel_id=1, source_target_pairs={{0,1},{1,0},{2,3},{3,2},{4,5},{5,4},{6,7},{7,6},{8,9},{9,8},{10,11... | collective-permute-start | bytes 786440 | tf_op jit(solution)/shard_map/ppermute | solution.py:285
  25.1 4.2 %copy-start.1 = (bf16[1,2048,512]{2,1,0:T(8,128)(2,1)S(1)}, bf16[1,2048,512]{2,1,0:T(8,128)(2,1)}, u32[]{:S(2)}) copy-start(bf16[1,2048,512]{2,1,0:T(8,128)(2,1)} %down_own.3) | copy-start | bytes 6291460
  31.4 14.9 %collective-permute-start.6 = (bf16[256,512]{1,0:T(8,128)(2,1)S(1)}, bf16[256,512]{1,0:T(8,128)(2,1)S(1)}, u32[]{:S(2)}, u32[]{:S(2)}) collective-permute-start(bf16[256,512]{1,0:T(8,128)(2,1)S(1)} %shard_map.84.state), channel_id=1, source_target_pairs={{1,2},{2,1},{3,4},{4,3},{5,6},{6,5},{7,8},{8,7},{9,10},{10,9},{11,... | collective-permute-start | bytes 786440 | tf_op jit(solution)/shard_map/ppermute | solution.py:282
  37.2 9.5 %collective-permute-start.5 = (bf16[256,512]{1,0:T(8,128)(2,1)S(1)}, bf16[256,512]{1,0:T(8,128)(2,1)S(1)}, u32[]{:S(2)}, u32[]{:S(2)}) collective-permute-start(bf16[256,512]{1,0:T(8,128)(2,1)S(1)} %shard_map.84.state), channel_id=1, source_target_pairs={{0,1},{1,0},{2,3},{3,2},{4,5},{5,4},{6,7},{7,6},{8,9},{9,8},{10,11... | collective-permute-start | bytes 786440 | tf_op jit(solution)/shard_map/ppermute | solution.py:285

commit v3 on v2

v3 whole, which is shorter than its diff:
```python
import functools

import jax
import jax.numpy as jnp
from jax import lax
from jax.experimental import pallas as pl
from jax.experimental.pallas import tpu as pltpu
from jax.sharding import PartitionSpec as P


HEADS = 8
HEAD = 64
D = 512
PATCH = 128
LINKS = 3
PAIRS = HEADS // 2
EPS = 1e-05
FF = 2048
WIDTH = 1024
LIMIT = 16 << 20
BF16 = jnp.bfloat16
F32 = jnp.float32

QKV, OUT, FIRST = 0, 3, 4


def dot(a, b):
    return jnp.dot(a, b, preferred_element_type=F32)


def normalize(values):
    center = jnp.mean(values, axis=-1, keepdims=True)
    shifted = values - center
    spread = jnp.mean(shifted * shifted, axis=-1, keepdims=True)
    return (shifted * lax.rsqrt(spread + EPS)).astype(BF16)


def gelu(x):
    return 0.5 * x * (1.0 + lax.erf(x * (0.5**0.5)))


def copies_of(pairs, sem):
    return [pltpu.make_async_copy(a, b, sem.at[i]) for i, (a, b) in enumerate(pairs)]


def arrange_kernel(hits_hbm, order_hbm, w_qkv, w_out, ordered, sent, packed, hits, order, sem):
    event = lax.axis_index("section")
    pairs = [(hits_hbm.at[0], hits), (order_hbm.at[event], order)]
    for i in range(3):
        pairs.append((w_qkv.at[0, :, pl.ds(i * D, D)], packed.at[QKV + i]))
    pairs.append((w_out.at[0], packed.at[OUT]))
    copies = copies_of(pairs, sem)
    for copy in copies:
        copy.start()
    copies[0].wait()
    copies[1].wait()
    rows = hits.shape[0]
    source_row = lax.broadcasted_iota(jnp.int32, (rows, rows), 0)
    chosen = jnp.where(source_row == order[...], 1.0, 0.0).T.astype(BF16)
    state = dot(chosen, hits[...]).astype(BF16)
    ordered[...] = state
    sent[...] = normalize(state.astype(F32))
    for copy in copies[2:]:
        copy.wait()


def arrange(hits, order, w_qkv, w_out):
    rows = hits.shape[1]
    vmem = pl.BlockSpec(memory_space=pltpu.VMEM)
    args = [pltpu.with_memory_space_constraint(a, pltpu.HBM) for a in (hits, order, w_qkv, w_out)]
    return pl.pallas_call(
        arrange_kernel,
        name="arrange",
        out_shape=(
            jax.ShapeDtypeStruct((rows, D), BF16),
            jax.ShapeDtypeStruct((rows, D), BF16),
            jax.ShapeDtypeStruct((FIRST, D, D), BF16),
        ),
        in_specs=[pl.BlockSpec(memory_space=pltpu.HBM)] * 4,
        out_specs=(vmem,) * 3,
        scratch_shapes=[
            pltpu.VMEM((rows, D), BF16),
            pltpu.VMEM((1, rows), jnp.int32),
            pltpu.SemaphoreType.DMA((FIRST + 2,)),
        ],
        compiler_params=pltpu.CompilerParams(vmem_limit_bytes=20 << 20),
        cost_estimate=pl.CostEstimate(
            flops=2 * rows * rows * D, bytes_accessed=4 << 20, transcendentals=0
        ),
    )(*args)


def with_weights(block, own, came, body):
    section = lax.axis_index("section")

    @pl.when(section == block)
    def _():
        body(*own)

    @pl.when(section != block)
    def _():
        body(*came)


def turned(values, patch, pair):
    part = values[patch * PATCH : (patch + 1) * PATCH, pair * 128 : (pair + 1) * 128]
    return part.T.astype(BF16)


def prepare_kernel(block, sent, own, came, queries, keys, values):
    low = lax.broadcasted_iota(jnp.int32, (PATCH, 128), 1) < HEAD
    scale = jnp.asarray(HEAD**-0.5, BF16)
    low_scale = jnp.where(low, scale, 0.0).astype(BF16)
    high_scale = jnp.where(low, 0.0, scale).astype(BF16)

    def body(weights):
        normed = sent[...]
        query = dot(normed, weights[QKV]).astype(BF16)
        keys[...] = dot(normed, weights[QKV + 1]).astype(BF16)
        value = dot(normed, weights[QKV + 2])
        for patch in range(sent.shape[0] // PATCH):
            for pair in range(PAIRS):
                part = query[patch * PATCH : (patch + 1) * PATCH, pair * 128 : (pair + 1) * 128]
                queries[patch, pair, 0:PATCH, :] = part * low_scale
                queries[patch, pair, PATCH : 2 * PATCH, :] = part * high_scale
                values[patch, pair] = turned(value, patch, pair)

    with_weights(block, (own,), (came,), body)


def prepare(block, sent, own, came):
    rows = sent.shape[0]
    patches = rows // PATCH
    vmem = pl.BlockSpec(memory_space=pltpu.VMEM)
    return pl.pallas_call(
        functools.partial(prepare_kernel, block),
        out_shape=(
            jax.ShapeDtypeStruct((patches, PAIRS, 2 * PATCH, 128), BF16),
            jax.ShapeDtypeStruct((rows, D), BF16),
            jax.ShapeDtypeStruct((patches, PAIRS, 128, PATCH), BF16),
        ),
        in_specs=[vmem] * 3,
        out_specs=(vmem,) * 3,
        compiler_params=pltpu.CompilerParams(vmem_limit_bytes=LIMIT),
        cost_estimate=pl.CostEstimate(
            flops=6 * rows * D * D, bytes_accessed=4 << 20, transcendentals=0
        ),
    )(sent, own, came)


def attend_kernel(
    block,
    links,
    counts,
    state,
    queries,
    own_keys,
    own_values,
    near_a,
    near_b,
    own,
    came,
    middle,
    keys,
    values,
    scores,
    tops,
    totals,
    attended,
    sem,
):
    event = lax.axis_index("section")
    region = lax.axis_index("region")
    regions = counts.shape[1]
    rows = state.shape[0]
    patches = rows // PATCH
    bring = copies_of(
        [(own_keys, keys.at[pl.ds(0, rows)]), (own_values, values.at[pl.ds(0, patches)])], sem
    )
    for copy in bring:
        copy.start()
    even = lax.rem(region, 2) == 0
    region_a = jnp.where(even, region + 1, region - 1)
    region_b = jnp.where(even, region - 1, region + 1)
    count_own = counts[event, region]
    count_a = counts[event, jnp.clip(region_a, 0, regions - 1)]
    count_b = counts[event, jnp.clip(region_b, 0, regions - 1)]
    key_row = lax.broadcasted_iota(jnp.int32, (PATCH, 2 * PATCH), 0)
    ones = jnp.ones((16, LINKS * PATCH), BF16)

    def body(weights):
        normed = jnp.concatenate([near_a[...], near_b[...]], axis=0)
        keys[rows : 3 * rows, :] = dot(normed, weights[QKV + 1]).astype(BF16)
        value = dot(normed, weights[QKV + 2])
        for patch in range(2 * patches):
            for pair in range(PAIRS):
                values[patches + patch, pair] = turned(value, patch, pair)
        for copy in bring:
            copy.wait()
        slots = []
        for patch in range(patches):
            valid = []
            for link in range(LINKS):
                linked = links[event, patch, link]
                owner = lax.div(linked, patches)
                half = lax.rem(linked, patches)
                base = jnp.where(owner == region, 0, jnp.where(owner == region_a, 1, 2))
                count = jnp.where(base == 0, count_own, jnp.where(base == 1, count_a, count_b))
                slots.append(base * patches + half)
                valid.append(key_row < count - half * PATCH)
            for pair in range(PAIRS):
                unit = patch * PAIRS + pair
                query = queries[patch, pair]
                top = None
                for link in range(LINKS):
                    start = pl.multiple_of(slots[patch * LINKS + link] * PATCH, PATCH)
                    score = lax.dot_general(
                        keys[pl.ds(start, PATCH), pair * 128 : (pair + 1) * 128],
                        query,
                        (((1,), (1,)), ((), ())),
                        preferred_element_type=F32,
                    )
                    score = jnp.where(valid[link], score, -1e30)
                    scores[unit, link * PATCH : (link + 1) * PATCH, :] = score
                    top = score if top is None else jnp.maximum(top, score)
                tops[unit] = jnp.broadcast_to(jnp.max(top, axis=0, keepdims=True), (8, 2 * PATCH))
        for patch in range(patches):
            for pair in range(PAIRS):
                unit = patch * PAIRS + pair
                weighed = jnp.exp(scores[unit] - tops[unit, 0:1, :]).astype(BF16)
                taken = jnp.concatenate(
                    [values[slot, pair] for slot in slots[patch * LINKS : (patch + 1) * LINKS]],
                    axis=1,
                )
                totals[unit] = dot(jnp.concatenate([taken, ones], axis=0), weighed)
        for patch in range(patches):
            for pair in range(PAIRS):
                unit = patch * PAIRS + pair
                share = 1.0 / totals[unit, 128:129, :]
                whole = jnp.concatenate(
                    [
                        totals[unit, 0:HEAD, 0:PATCH] * share[:, 0:PATCH],
                        totals[unit, HEAD:128, PATCH:] * share[:, PATCH:],
                    ],
                    axis=0,
                )
                attended[
                    patch * PATCH : (patch + 1) * PATCH, pair * 128 : (pair + 1) * 128
                ] = whole.T.astype(BF16)
        middle[...] = (state[...].astype(F32) + dot(attended[...], weights[OUT])).astype(BF16)

    with_weights(block, (own,), (came,), body)


def attend(block, links, counts, state, queries, keys, values, near_a, near_b, own, came):
    rows = state.shape[0]
    patches = rows // PATCH
    vmem = pl.BlockSpec(memory_space=pltpu.VMEM)
    smem = pl.BlockSpec(memory_space=pltpu.SMEM)
    return pl.pallas_call(
        functools.partial(attend_kernel, block),
        out_shape=jax.ShapeDtypeStruct((rows, D), BF16),
        in_specs=[smem, smem] + [vmem] * 8,
        out_specs=vmem,
        scratch_shapes=[
            pltpu.VMEM((3 * rows, D), BF16),
            pltpu.VMEM((3 * patches, PAIRS, 128, PATCH), BF16),
            pltpu.VMEM((patches * PAIRS, LINKS * PATCH, 2 * PATCH), F32),
            pltpu.VMEM((patches * PAIRS, 8, 2 * PATCH), F32),
            pltpu.VMEM((patches * PAIRS, 144, 2 * PATCH), F32),
            pltpu.VMEM((rows, D), BF16),
            pltpu.SemaphoreType.DMA((2,)),
        ],
        compiler_params=pltpu.CompilerParams(vmem_limit_bytes=LIMIT),
        cost_estimate=pl.CostEstimate(
            flops=10**9, bytes_accessed=4 << 20, transcendentals=8 * 10**5
        ),
    )(links, counts, state, queries, keys, values, near_a, near_b, own, came)


def feed_kernel(
    block, last, counts, middle_ref, up_own, down_own, up_came, down_came, result, *sent
):
    def body(up, down):
        middle = middle_ref[...].astype(F32)
        normed = normalize(middle)
        total = middle
        for part in range(0, FF, WIDTH):
            hidden = gelu(dot(normed, up[0, :, part : part + WIDTH])).astype(BF16)
            total = total + dot(hidden, down[0, part : part + WIDTH, :])
        total = total.astype(BF16)
        if last:
            count = counts[lax.axis_index("section"), lax.axis_index("region")]
            row = lax.broadcasted_iota(jnp.int32, total.shape, 0)
            total = jnp.where(row < count, total.astype(F32), 0.0).astype(BF16)
        else:
            sent[0][...] = normalize(total.astype(F32))
        result[...] = total

    with_weights(block, (up_own, down_own), (up_came, down_came), body)


def feed(block, last, counts, middle, *weights):
    rows = middle.shape[0]
    outputs = 1 if last else 2
    vmem = pl.BlockSpec(memory_space=pltpu.VMEM)
    smem = pl.BlockSpec(memory_space=pltpu.SMEM)
    return pl.pallas_call(
        functools.partial(feed_kernel, block, last),
        out_shape=(jax.ShapeDtypeStruct((rows, D), BF16),) * outputs,
        in_specs=[smem] + [vmem] * 5,
        out_specs=(vmem,) * outputs,
        compiler_params=pltpu.CompilerParams(vmem_limit_bytes=LIMIT),
        cost_estimate=pl.CostEstimate(
            flops=4 * rows * FF * D, bytes_accessed=5 << 20, transcendentals=10**6
        ),
    )(counts, middle, *weights)


def per_device(hits, order, links, counts, w_qkv, w_out, w_up, w_down):
    regions = counts.shape[1]
    pairs_a = [(i, i ^ 1) for i in range(regions)]
    pairs_b = []
    for i in range(1, regions - 1, 2):
        pairs_b += [(i, i + 1), (i + 1, i)]
    swap = [(0, 1), (1, 0)]
    state, sent, own = arrange(hits, order, w_qkv, w_out)
    for block in range(2):
        near_b = lax.ppermute(sent, "region", pairs_b)
        if block == 0:
            came = lax.ppermute(own, "section", swap)
        near_a = lax.ppermute(sent, "region", pairs_a)
        if block == 0:
            up_came = lax.ppermute(w_up, "section", swap)
            down_came = lax.ppermute(w_down, "section", swap)
            second = (w_up, w_down, up_came, down_came)
        queries, keys, values = prepare(block, sent, own, came)
        middle = attend(
            block,
            links,
            counts,
            state,
            queries,
            keys,
            values,
            near_a,
            near_b,
            own,
            came,
        )
        state, *sent = feed(block, block == 1, counts, middle, *second)
        sent = sent[0] if sent else None
    return state[None]


def solution(mesh):
    in_specs = (
        P("section", "region", None),
        P(None, "region", None),
        P(None, "region", None),
        P(),
        P("section", None, None),
        P("section", None, None),
        P("section", None, None),
        P("section", None, None),
    )
    out_specs = P("section", "region", None)
    return jax.shard_map(
        per_device, mesh=mesh, in_specs=in_specs, out_specs=out_specs, check_vma=False
    )
```

time: 54.1 us -> 52 us (0.961)
  Pallas kernels: 16.8 us -> 14.5 us
    pallas_call x2, Pallas kernels: 8.43 us -> 6.15 us  [attend(): pl.pallas_call(functools.partial(attend_kernel, block), out_shape=jax.Sha...]
  transfers between devices with their start and end apart: 7 -> 7, of which waited for: 4 -> 4; matrix products, arithmetic and copies ran while one was open for 0% -> 0% of each run, Pallas kernels for 11% -> 8%
where the time goes in v3:
time: 52 us; the launch traced here: 51.7 us
  starting transfers between devices  22.5 us (43%)
  waiting for transfers between devices  14.6 us (28%)
  Pallas kernels  14.5 us (28%)
    ppermute x2, waiting for transfers between devices, per_device(): near_b = lax.ppermute(sent, 'region', pairs_b)  13.3 us
    ppermute x2, starting transfers between devices, per_device(): near_b = lax.ppermute(sent, 'region', pairs_b)  12.4 us
    pallas_call x2, Pallas kernels, attend(): pl.pallas_call(functools.partial(attend_kernel, block), out_shape=jax.Sha...  6.15 us
    pallas_call x2, Pallas kernels, feed(): pl.pallas_call(functools.partial(feed_kernel, block, last), out_shape=(ja...  5.16 us
    ppermute x2, starting transfers between devices, per_device(): near_a = lax.ppermute(sent, 'region', pairs_a)  3.84 us
    ppermute x1, starting transfers between devices, per_device(): up_came = lax.ppermute(w_up, 'section', swap)  2.41 us
    ppermute x1, starting transfers between devices, per_device(): down_came = lax.ppermute(w_down, 'section', swap)  1.92 us
    ppermute x1, starting transfers between devices, per_device(): came = lax.ppermute(own, 'section', swap)  1.92 us
  transfers between devices with their start and end apart: 7, of which 4 were waited for; matrix products, arithmetic and copies ran while one was open for 0% of the time, Pallas kernels for 8%

profile of v3, /device:TPU:256, one launch (start us, length us, event | category | flops | bytes accessed | tf_op | source)
XLA Modules:
  0.0 51.7 jit_solution(15168477760322849430)
XLA Ops:
  0.0 0.0 copy-start
  0.0 1.8 %arrange.1 = (bf16[256,512]{1,0:T(8,128)(2,1)S(1)}, bf16[256,512]{1,0:T(8,128)(2,1)S(1)}, bf16[4,512,512]{2,1,0:T(8,128)(2,1)S(1)}) custom-call(bf16[1,256,512]{2,1,0:T(8,128)(2,1)} %hits_hbm.1, s32[2,1,256]{2,1,0:T(1,128)} %order_hbm.1, bf16[1,512,1536]{2,1,0:T(8,128)(2,1)} %w_qkv.1, bf16[1,512,512]{2,1,0:T(8,128)(2,1)} %w_out.1), custom_call_target="tpu_custom_call" | custom-call | flops 67108864 | bytes 4194304 | tf_op jit(solution)/shard_map/arrange/pallas_call | solution.py:71
  1.8 1.9 %collective-permute-start = (bf16[4,512,512]{2,1,0:T(8,128)(2,1)S(1)}, bf16[4,512,512]{2,1,0:T(8,128)(2,1)S(1)}, u32[]{:S(2)}, u32[]{:S(2)}) collective-permute-start(bf16[4,512,512]{2,1,0:T(8,128)(2,1)S(1)} %get-tuple-element.18.own), channel_id=1, source_target_pairs={{0,256},{256,0},{1,257},{257,1},{2,258},{258,2},{3,259},{259,3},{4... | collective-permute-start | bytes 6291464 | tf_op jit(solution)/shard_map/ppermute | solution.py:331
  3.8 0.0 copy-done
  3.8 2.4 %collective-permute-start.3 = (bf16[1,512,2048]{2,1,0:T(8,128)(2,1)S(1)}, bf16[1,512,2048]{2,1,0:T(8,128)(2,1)S(1)}, u32[]{:S(2)}, u32[]{:S(2)}) collective-permute-start(bf16[1,512,2048]{2,1,0:T(8,128)(2,1)S(1)} %copy-done), channel_id=1, source_target_pairs={{0,256},{256,0},{1,257},{257,1},{2,258},{258,2},{3,259},{259,3},{4... | collective-permute-start | bytes 6291464 | tf_op jit(solution)/shard_map/ppermute | solution.py:334
  6.2 1.9 %collective-permute-start.4 = (bf16[1,2048,512]{2,1,0:T(8,128)(2,1)}, bf16[1,2048,512]{2,1,0:T(8,128)(2,1)S(1)}, u32[]{:S(2)}, u32[]{:S(2)}) collective-permute-start(bf16[1,2048,512]{2,1,0:T(8,128)(2,1)} %down_own.3), channel_id=1, source_target_pairs={{0,256},{256,0},{1,257},{257,1},{2,258},{258,2},{3,259},{259,3},{4... | collective-permute-start | bytes 6291464 | tf_op jit(solution)/shard_map/ppermute | solution.py:335
  8.1 0.0 copy-start.2
  8.1 0.0 copy-start.3
  8.1 6.7 %collective-permute-start.2 = (bf16[256,512]{1,0:T(8,128)(2,1)S(1)}, bf16[256,512]{1,0:T(8,128)(2,1)S(1)}, u32[]{:S(2)}, u32[]{:S(2)}) collective-permute-start(bf16[256,512]{1,0:T(8,128)(2,1)S(1)} %get-tuple-element.17.sent), channel_id=1, source_target_pairs={{1,2},{2,1},{3,4},{4,3},{5,6},{6,5},{7,8},{8,7},{9,10},{10,9},{11,... | collective-permute-start | bytes 786440 | tf_op jit(solution)/shard_map/ppermute | solution.py:329
  14.8 1.9 %collective-permute-start.1 = (bf16[256,512]{1,0:T(8,128)(2,1)S(1)}, bf16[256,512]{1,0:T(8,128)(2,1)S(1)}, u32[]{:S(2)}, u32[]{:S(2)}) collective-permute-start(bf16[256,512]{1,0:T(8,128)(2,1)S(1)} %get-tuple-element.17.sent), channel_id=1, source_target_pairs={{0,1},{1,0},{2,3},{3,2},{4,5},{5,4},{6,7},{7,6},{8,9},{9,8},{10,11... | collective-permute-start | bytes 786440 | tf_op jit(solution)/shard_map/ppermute | solution.py:332
  16.7 0.0 collective-permute-done.came
  16.7 0.7 %shard_map.82 = (bf16[2,4,256,128]{3,2,1,0:T(8,128)(2,1)S(1)}, bf16[256,512]{1,0:T(8,128)(2,1)S(1)}, bf16[2,4,128,128]{3,2,1,0:T(8,128)(2,1)S(1)}) custom-call(bf16[256,512]{1,0:T(8,128)(2,1)S(1)} %get-tuple-element.17.sent, bf16[4,512,512]{2,1,0:T(8,128)(2,1)S(1)} %get-tuple-element.18.own, bf16[4,512,512]{2,1,0:T(8,128)(2,1)S(1)} %collective-permute-done.came), custom_call_target="tpu_custom_call" | custom-call | flops 402653184 | bytes 4194304 | tf_op jit(solution)/shard_map/pallas_call | solution.py:135
  17.4 6.7 %collective-permute-done.2.near_b = bf16[256,512]{1,0:T(8,128)(2,1)S(1)} collective-permute-done((bf16[256,512]{1,0:T(8,128)(2,1)S(1)}, bf16[256,512]{1,0:T(8,128)(2,1)S(1)}, u32[]{:S(2)}, u32[]{:S(2)}) %collective-permute-start.2) | collective-permute-done | bytes 262176 | tf_op jit(solution)/shard_map/ppermute | solution.py:329
  24.2 1.0 %collective-permute-done.1.near_a = bf16[256,512]{1,0:T(8,128)(2,1)S(1)} collective-permute-done((bf16[256,512]{1,0:T(8,128)(2,1)S(1)}, bf16[256,512]{1,0:T(8,128)(2,1)S(1)}, u32[]{:S(2)}, u32[]{:S(2)}) %collective-permute-start.1) | collective-permute-done | bytes 262176 | tf_op jit(solution)/shard_map/ppermute | solution.py:332
  25.1 0.0 copy-done.2
  25.1 0.0 copy-done.3
  25.1 0.0 copy-start.1
  25.1 3.0 %shard_map.83.middle_ref = bf16[256,512]{1,0:T(8,128)(2,1)S(1)} custom-call(s32[2,2,3]{2,1,0:T(2,128)S(1)} %copy-done.3, s32[2,256]{1,0:T(2,128)S(1)} %copy-done.2, bf16[256,512]{1,0:T(8,128)(2,1)S(1)} %get-tuple-element.16.state, bf16[2,4,256,128]{3,2,1,0:T(8,128)(2,1)S(1)} %get-tuple-element.19.queries, bf16[256,512]{1,0:T(8,128)(2,1)S(1)} %get-tuple-element.20.own_keys, ...), custom_call_target="tpu_custom_call" | custom-call | flops 1000000000 | bytes 4194304 | tf_op jit(solution)/shard_map/pallas_call | solution.py:260
  28.1 0.0 collective-permute-done.3.up_came
  28.1 0.0 collective-permute-done.4.down_came
  28.1 0.0 copy-done.1
  28.2 2.3 %shard_map.84 = (bf16[256,512]{1,0:T(8,128)(2,1)S(1)}, bf16[256,512]{1,0:T(8,128)(2,1)S(1)}) custom-call(s32[2,256]{1,0:T(2,128)S(1)} %copy-done.2, bf16[256,512]{1,0:T(8,128)(2,1)S(1)} %shard_map.83.middle_ref, bf16[1,512,2048]{2,1,0:T(8,128)(2,1)S(1)} %copy-done, bf16[1,2048,512]{2,1,0:T(8,128)(2,1)S(1)} %copy-done.1, ...), custom_call_target="tpu_custom_call" | custom-call | flops 1073741824 | bytes 5242880 | tf_op jit(solution)/shard_map/pallas_call | solution.py:308
  30.5 5.7 %collective-permute-start.6 = (bf16[256,512]{1,0:T(8,128)(2,1)S(1)}, bf16[256,512]{1,0:T(8,128)(2,1)S(1)}, u32[]{:S(2)}, u32[]{:S(2)}) collective-permute-start(bf16[256,512]{1,0:T(8,128)(2,1)S(1)} %get-tuple-element.23.sent), channel_id=1, source_target_pairs={{1,2},{2,1},{3,4},{4,3},{5,6},{6,5},{7,8},{8,7},{9,10},{10,9},{11,... | collective-permute-start | bytes 786440 | tf_op jit(solution)/shard_map/ppermute | solution.py:329
  36.2 1.9 %collective-permute-start.5 = (bf16[256,512]{1,0:T(8,128)(2,1)S(1)}, bf16[256,512]{1,0:T(8,128)(2,1)S(1)}, u32[]{:S(2)}, u32[]{:S(2)}) collective-permute-start(bf16[256,512]{1,0:T(8,128)(2,1)S(1)} %get-tuple-element.23.sent), channel_id=1, source_target_pairs={{0,1},{1,0},{2,3},{3,2},{4,5},{5,4},{6,7},{7,6},{8,9},{9,8},{10,11... | collective-permute-start | bytes 786440 | tf_op jit(solution)/shard_map/ppermute | solution.py:332
  38.1 0.7 %shard_map.85 = (bf16[2,4,256,128]{3,2,1,0:T(8,128)(2,1)S(1)}, bf16[256,512]{1,0:T(8,128)(2,1)S(1)}, bf16[2,4,128,128]{3,2,1,0:T(8,128)(2,1)S(1)}) custom-call(bf16[256,512]{1,0:T(8,128)(2,1)S(1)} %get-tuple-element.23.sent, bf16[4,512,512]{2,1,0:T(8,128)(2,1)S(1)} %get-tuple-element.18.own, bf16[4,512,512]{2,1,0:T(8,128)(2,1)S(1)} %collective-permute-done.came), custom_call_target="tpu_custom_call" | custom-call | flops 402653184 | bytes 4194304 | tf_op jit(solution)/shard_map/pallas_call | solution.py:135
  38.8 6.5 %collective-permute-done.6.near_b = bf16[256,512]{1,0:T(8,128)(2,1)S(1)} collective-permute-done((bf16[256,512]{1,0:T(8,128)(2,1)S(1)}, bf16[256,512]{1,0:T(8,128)(2,1)S(1)}, u32[]{:S(2)}, u32[]{:S(2)}) %collective-permute-start.6) | collective-permute-done | bytes 262176 | tf_op jit(solution)/shard_map/ppermute | solution.py:329
  45.3 0.3 collective-permute-done.5.near_a
  45.6 3.2 %shard_map.86.middle_ref = bf16[256,512]{1,0:T(8,128)(2,1)S(1)} custom-call(s32[2,2,3]{2,1,0:T(2,128)S(1)} %copy-done.3, s32[2,256]{1,0:T(2,128)S(1)} %copy-done.2, bf16[256,512]{1,0:T(8,128)(2,1)S(1)} %get-tuple-element.22.state, bf16[2,4,256,128]{3,2,1,0:T(8,128)(2,1)S(1)} %get-tuple-element.24.queries, bf16[256,512]{1,0:T(8,128)(2,1)S(1)} %get-tuple-element.25.own_keys, ...), custom_call_target="tpu_custom_call" | custom-call | flops 1000000000 | bytes 4194304 | tf_op jit(solution)/shard_map/pallas_call | solution.py:260
  48.8 2.8 %shard_map.87 = bf16[256,512]{1,0:T(8,128)(2,1)} custom-call(s32[2,256]{1,0:T(2,128)S(1)} %copy-done.2, bf16[256,512]{1,0:T(8,128)(2,1)S(1)} %shard_map.86.middle_ref, bf16[1,512,2048]{2,1,0:T(8,128)(2,1)S(1)} %copy-done, bf16[1,2048,512]{2,1,0:T(8,128)(2,1)S(1)} %copy-done.1, bf16[1,512,2048]{2,1,0:T(8,128)(2,1)S(1)} %collective-permute-done.3.up_came, ...), custom_call_target="tpu_custom_call" | custom-call | flops 1073741824 | bytes 5242880 | tf_op jit(solution)/shard_map/pallas_call | solution.py:308
Async XLA Ops:
  0.0 3.8 %copy-start = (bf16[1,512,2048]{2,1,0:T(8,128)(2,1)S(1)}, bf16[1,512,2048]{2,1,0:T(8,128)(2,1)}, u32[]{:S(2)}) copy-start(bf16[1,512,2048]{2,1,0:T(8,128)(2,1)} %up_own.3) | copy-start | bytes 6291460
  1.8 14.9 %collective-permute-start = (bf16[4,512,512]{2,1,0:T(8,128)(2,1)S(1)}, bf16[4,512,512]{2,1,0:T(8,128)(2,1)S(1)}, u32[]{:S(2)}, u32[]{:S(2)}) collective-permute-start(bf16[4,512,512]{2,1,0:T(8,128)(2,1)S(1)} %get-tuple-element.18.own), channel_id=1, source_target_pairs={{0,256},{256,0},{1,257},{257,1},{2,258},{258,2},{3,259},{259,3},{4... | collective-permute-start | bytes 6291464 | tf_op jit(solution)/shard_map/ppermute | solution.py:331
  3.8 24.4 %collective-permute-start.3 = (bf16[1,512,2048]{2,1,0:T(8,128)(2,1)S(1)}, bf16[1,512,2048]{2,1,0:T(8,128)(2,1)S(1)}, u32[]{:S(2)}, u32[]{:S(2)}) collective-permute-start(bf16[1,512,2048]{2,1,0:T(8,128)(2,1)S(1)} %copy-done), channel_id=1, source_target_pairs={{0,256},{256,0},{1,257},{257,1},{2,258},{258,2},{3,259},{259,3},{4... | collective-permute-start | bytes 6291464 | tf_op jit(solution)/shard_map/ppermute | solution.py:334
  6.2 22.0 %collective-permute-start.4 = (bf16[1,2048,512]{2,1,0:T(8,128)(2,1)}, bf16[1,2048,512]{2,1,0:T(8,128)(2,1)S(1)}, u32[]{:S(2)}, u32[]{:S(2)}) collective-permute-start(bf16[1,2048,512]{2,1,0:T(8,128)(2,1)} %down_own.3), channel_id=1, source_target_pairs={{0,256},{256,0},{1,257},{257,1},{2,258},{258,2},{3,259},{259,3},{4... | collective-permute-start | bytes 6291464 | tf_op jit(solution)/shard_map/ppermute | solution.py:335
  8.1 17.0 %copy-start.2 = (s32[2,256]{1,0:T(2,128)S(1)}, s32[2,256]{1,0:T(2,128)}, u32[]{:S(2)}) copy-start(s32[2,256]{1,0:T(2,128)} %counts.7) | copy-start | bytes 6148
  8.1 17.0 %copy-start.3 = (s32[2,2,3]{2,1,0:T(2,128)S(1)}, s32[2,2,3]{2,1,0:T(2,128)}, u32[]{:S(2)}) copy-start(s32[2,2,3]{2,1,0:T(2,128)} %links.3) | copy-start | bytes 148
  8.1 16.0 %collective-permute-start.2 = (bf16[256,512]{1,0:T(8,128)(2,1)S(1)}, bf16[256,512]{1,0:T(8,128)(2,1)S(1)}, u32[]{:S(2)}, u32[]{:S(2)}) collective-permute-start(bf16[256,512]{1,0:T(8,128)(2,1)S(1)} %get-tuple-element.17.sent), channel_id=1, source_target_pairs={{1,2},{2,1},{3,4},{4,3},{5,6},{6,5},{7,8},{8,7},{9,10},{10,9},{11,... | collective-permute-start | bytes 786440 | tf_op jit(solution)/shard_map/ppermute | solution.py:329
  14.8 10.3 %collective-permute-start.1 = (bf16[256,512]{1,0:T(8,128)(2,1)S(1)}, bf16[256,512]{1,0:T(8,128)(2,1)S(1)}, u32[]{:S(2)}, u32[]{:S(2)}) collective-permute-start(bf16[256,512]{1,0:T(8,128)(2,1)S(1)} %get-tuple-element.17.sent), channel_id=1, source_target_pairs={{0,1},{1,0},{2,3},{3,2},{4,5},{5,4},{6,7},{7,6},{8,9},{9,8},{10,11... | collective-permute-start | bytes 786440 | tf_op jit(solution)/shard_map/ppermute | solution.py:332
  25.1 3.0 %copy-start.1 = (bf16[1,2048,512]{2,1,0:T(8,128)(2,1)S(1)}, bf16[1,2048,512]{2,1,0:T(8,128)(2,1)}, u32[]{:S(2)}) copy-start(bf16[1,2048,512]{2,1,0:T(8,128)(2,1)} %down_own.3) | copy-start | bytes 6291460
  30.5 14.9 %collective-permute-start.6 = (bf16[256,512]{1,0:T(8,128)(2,1)S(1)}, bf16[256,512]{1,0:T(8,128)(2,1)S(1)}, u32[]{:S(2)}, u32[]{:S(2)}) collective-permute-start(bf16[256,512]{1,0:T(8,128)(2,1)S(1)} %get-tuple-element.23.sent), channel_id=1, source_target_pairs={{1,2},{2,1},{3,4},{4,3},{5,6},{6,5},{7,8},{8,7},{9,10},{10,9},{11,... | collective-permute-start | bytes 786440 | tf_op jit(solution)/shard_map/ppermute | solution.py:329
  36.2 9.4 %collective-permute-start.5 = (bf16[256,512]{1,0:T(8,128)(2,1)S(1)}, bf16[256,512]{1,0:T(8,128)(2,1)S(1)}, u32[]{:S(2)}, u32[]{:S(2)}) collective-permute-start(bf16[256,512]{1,0:T(8,128)(2,1)S(1)} %get-tuple-element.23.sent), channel_id=1, source_target_pairs={{0,1},{1,0},{2,3},{3,2},{4,5},{5,4},{6,7},{7,6},{8,9},{9,8},{10,11... | collective-permute-start | bytes 786440 | tf_op jit(solution)/shard_map/ppermute | solution.py:332

commit v4 on v3

--- a/solution.py
+++ b/solution.py
@@ -150,8 +150,8 @@
 
 def attend_kernel(
     block,
-    links,
-    counts,
+    links_in,
+    counts_in,
     state,
     queries,
     own_keys,
@@ -167,6 +167,8 @@
     tops,
     totals,
     attended,
+    links,
+    counts,
     sem,
 ):
     event = lax.axis_index("section")
@@ -175,28 +177,34 @@
     rows = state.shape[0]
     patches = rows // PATCH
     bring = copies_of(
-        [(own_keys, keys.at[pl.ds(0, rows)]), (own_values, values.at[pl.ds(0, patches)])], sem
+        [
+            (links_in, links),
+            (counts_in, counts),
+            (own_keys, keys.at[pl.ds(0, rows)]),
+            (own_values, values.at[pl.ds(0, patches)]),
+        ],
+        sem,
     )
     for copy in bring:
         copy.start()
     even = lax.rem(region, 2) == 0
     region_a = jnp.where(even, region + 1, region - 1)
     region_b = jnp.where(even, region - 1, region + 1)
-    count_own = counts[event, region]
-    count_a = counts[event, jnp.clip(region_a, 0, regions - 1)]
-    count_b = counts[event, jnp.clip(region_b, 0, regions - 1)]
     key_row = lax.broadcasted_iota(jnp.int32, (PATCH, 2 * PATCH), 0)
     ones = jnp.ones((16, LINKS * PATCH), BF16)
 
     def body(weights):
         normed = jnp.concatenate([near_a[...], near_b[...]], axis=0)
-        keys[rows : 3 * rows, :] = dot(normed, weights[QKV + 1]).astype(BF16)
         value = dot(normed, weights[QKV + 2])
         for patch in range(2 * patches):
             for pair in range(PAIRS):
                 values[patches + patch, pair] = turned(value, patch, pair)
+        keys[rows : 3 * rows, :] = dot(normed, weights[QKV + 1]).astype(BF16)
         for copy in bring:
             copy.wait()
+        count_own = counts[event, region]
+        count_a = counts[event, jnp.clip(region_a, 0, regions - 1)]
+        count_b = counts[event, jnp.clip(region_b, 0, regions - 1)]
         slots = []
         for patch in range(patches):
             valid = []
@@ -256,11 +264,11 @@
     rows = state.shape[0]
     patches = rows // PATCH
     vmem = pl.BlockSpec(memory_space=pltpu.VMEM)
-    smem = pl.BlockSpec(memory_space=pltpu.SMEM)
+    any_space = pl.BlockSpec(memory_space=pl.ANY)
     return pl.pallas_call(
         functools.partial(attend_kernel, block),
         out_shape=jax.ShapeDtypeStruct((rows, D), BF16),
-        in_specs=[smem, smem] + [vmem] * 8,
+        in_specs=[any_space] * 2 + [vmem] * 2 + [any_space] * 2 + [vmem] * 4,
         out_specs=vmem,
         scratch_shapes=[
             pltpu.VMEM((3 * rows, D), BF16),
@@ -269,7 +277,9 @@
             pltpu.VMEM((patches * PAIRS, 8, 2 * PATCH), F32),
             pltpu.VMEM((patches * PAIRS, 144, 2 * PATCH), F32),
             pltpu.VMEM((rows, D), BF16),
-            pltpu.SemaphoreType.DMA((2,)),
+            pltpu.SMEM(links.shape, jnp.int32),
+            pltpu.SMEM(counts.shape, jnp.int32),
+            pltpu.SemaphoreType.DMA((4,)),
         ],
         compiler_params=pltpu.CompilerParams(vmem_limit_bytes=LIMIT),
         cost_estimate=pl.CostEstimate(
@@ -278,9 +288,31 @@
     )(links, counts, state, queries, keys, values, near_a, near_b, own, came)
 
 
+def raise_kernel(block, middle, own, came, hidden):
+    def body(up):
+        normed = normalize(middle[...].astype(F32))
+        for part in range(0, FF, WIDTH):
+            here = slice(part, part + WIDTH)
+            hidden[:, here] = gelu(dot(normed, up[0, :, here])).astype(BF16)
+
+    with_weights(block, (own,), (came,), body)
+
+
+def lower_kernel(block, hidden, middle, own, came, result, sent):
+    def body(down):
+        total = (middle[...].astype(F32) + dot(hidden[...], down[0])).astype(BF16)
+        result[...] = total
+        sent[...] = normalize(total.astype(F32))
+
+    with_weights(block, (own,), (came,), body)
+
+
 def feed_kernel(
-    block, last, counts, middle_ref, up_own, down_own, up_came, down_came, result, *sent
+    block, counts_in, middle_ref, up_own, down_own, up_came, down_came, result, counts, sem
 ):
+    bring = pltpu.make_async_copy(counts_in, counts, sem)
+    bring.start()
+
     def body(up, down):
         middle = middle_ref[...].astype(F32)
         normed = normalize(middle)
@@ -288,28 +320,48 @@
         for part in range(0, FF, WIDTH):
             hidden = gelu(dot(normed, up[0, :, part : part + WIDTH])).astype(BF16)
             total = total + dot(hidden, down[0, part : part + WIDTH, :])
-        total = total.astype(BF16)
-        if last:
-            count = counts[lax.axis_index("section"), lax.axis_index("region")]
-            row = lax.broadcasted_iota(jnp.int32, total.shape, 0)
-            total = jnp.where(row < count, total.astype(F32), 0.0).astype(BF16)
-        else:
-            sent[0][...] = normalize(total.astype(F32))
-        result[...] = total
+        bring.wait()
+        count = counts[lax.axis_index("section"), lax.axis_index("region")]
+        row = lax.broadcasted_iota(jnp.int32, total.shape, 0)
+        result[...] = jnp.where(row < count, total, 0.0).astype(BF16)
 
     with_weights(block, (up_own, down_own), (up_came, down_came), body)
 
 
-def feed(block, last, counts, middle, *weights):
+def feed_parts(block, middle, up_own, down_own, up_came, down_came):
     rows = middle.shape[0]
-    outputs = 1 if last else 2
     vmem = pl.BlockSpec(memory_space=pltpu.VMEM)
-    smem = pl.BlockSpec(memory_space=pltpu.SMEM)
+    params = pltpu.CompilerParams(vmem_limit_bytes=LIMIT)
+    cost = pl.CostEstimate(
+        flops=2 * rows * FF * D, bytes_accessed=3 << 20, transcendentals=5 * 10**5
+    )
+    hidden = pl.pallas_call(
+        functools.partial(raise_kernel, block),
+        out_shape=jax.ShapeDtypeStruct((rows, FF), BF16),
+        in_specs=[vmem] * 3,
+        out_specs=vmem,
+        compiler_params=params,
+        cost_estimate=cost,
+    )(middle, up_own, up_came)
     return pl.pallas_call(
-        functools.partial(feed_kernel, block, last),
-        out_shape=(jax.ShapeDtypeStruct((rows, D), BF16),) * outputs,
-        in_specs=[smem] + [vmem] * 5,
-        out_specs=(vmem,) * outputs,
+        functools.partial(lower_kernel, block),
+        out_shape=(jax.ShapeDtypeStruct((rows, D), BF16),) * 2,
+        in_specs=[vmem] * 4,
+        out_specs=(vmem,) * 2,
+        compiler_params=params,
+        cost_estimate=cost,
+    )(hidden, middle, down_own, down_came)
+
+
+def feed(block, counts, middle, *weights):
+    rows = middle.shape[0]
+    vmem = pl.BlockSpec(memory_space=pltpu.VMEM)
+    return pl.pallas_call(
+        functools.partial(feed_kernel, block),
+        out_shape=jax.ShapeDtypeStruct((rows, D), BF16),
+        in_specs=[pl.BlockSpec(memory_space=pl.ANY)] + [vmem] * 5,
+        out_specs=vmem,
+        scratch_shapes=[pltpu.SMEM(counts.shape, jnp.int32), pltpu.SemaphoreType.DMA],
         compiler_params=pltpu.CompilerParams(vmem_limit_bytes=LIMIT),
         cost_estimate=pl.CostEstimate(
             flops=4 * rows * FF * D, bytes_accessed=5 << 20, transcendentals=10**6
@@ -348,8 +400,10 @@
             own,
             came,
         )
-        state, *sent = feed(block, block == 1, counts, middle, *second)
-        sent = sent[0] if sent else None
+        if block == 0:
+            state, sent = feed_parts(block, middle, *second)
+        else:
+            state = feed(block, counts, middle, *second)
     return state[None]
 
 

time: 52 us -> 50.4 us (0.969)
  Pallas kernels: 14.5 us -> 12.1 us
  local copies, waits for them, and re-layouts: 0.02 us -> 0.57 us
    pallas_call x2, Pallas kernels: 6.15 us -> 4.82 us  [attend(): pl.pallas_call(functools.partial(attend_kernel, block), out_shape=jax.Sha...]
    pallas_call x2 -> x3, Pallas kernels: 5.16 us -> 4.15 us  [the longest x1 2.25 us: feed(): pl.pallas_call(functools.partial(feed_kernel, block), out_shape=jax.Shape...]
    unnamed x8, local copies, waits for them, and re-layouts: 0.02 us -> 0.57 us
  transfers between devices with their start and end apart: 7 -> 7, of which waited for: 4 -> 4; matrix products, arithmetic and copies ran while one was open for 0% -> 0% of each run, Pallas kernels for 8% -> 9%
where the time goes in v4:
time: 50.4 us; the launch traced here: 50.1 us
  starting transfers between devices  22.5 us (45%)
  waiting for transfers between devices  14.6 us (29%)
  Pallas kernels  12.1 us (24%)
  local copies, waits for them, and re-layouts  0.57 us (1%)
    ppermute x2, waiting for transfers between devices, per_device(): near_b = lax.ppermute(sent, 'region', pairs_b)  13.3 us
    ppermute x2, starting transfers between devices, per_device(): near_b = lax.ppermute(sent, 'region', pairs_b)  12.4 us
    pallas_call x2, Pallas kernels, attend(): pl.pallas_call(functools.partial(attend_kernel, block), out_shape=jax.Sha...  4.82 us
    ppermute x2, starting transfers between devices, per_device(): near_a = lax.ppermute(sent, 'region', pairs_a)  3.84 us
    ppermute x1, starting transfers between devices, per_device(): up_came = lax.ppermute(w_up, 'section', swap)  2.41 us
    pallas_call x1, Pallas kernels, feed(): pl.pallas_call(functools.partial(feed_kernel, block), out_shape=jax.Shape...  2.25 us
    ppermute x1, starting transfers between devices, per_device(): down_came = lax.ppermute(w_down, 'section', swap)  1.92 us
    ppermute x1, starting transfers between devices, per_device(): came = lax.ppermute(own, 'section', swap)  1.92 us
  transfers between devices with their start and end apart: 7, of which 4 were waited for; matrix products, arithmetic and copies ran while one was open for 0% of the time, Pallas kernels for 9%

profile of v4, /device:TPU:256, one launch (start us, length us, event | category | flops | bytes accessed | tf_op | source)
XLA Modules:
  0.0 50.1 jit_solution(12145026431069532579)
XLA Ops:
  0.0 0.0 copy-start
  0.0 1.8 %arrange.1 = (bf16[256,512]{1,0:T(8,128)(2,1)S(1)}, bf16[256,512]{1,0:T(8,128)(2,1)S(1)}, bf16[4,512,512]{2,1,0:T(8,128)(2,1)S(1)}) custom-call(bf16[1,256,512]{2,1,0:T(8,128)(2,1)} %hits_hbm.1, s32[2,1,256]{2,1,0:T(1,128)} %order_hbm.1, bf16[1,512,1536]{2,1,0:T(8,128)(2,1)} %w_qkv.1, bf16[1,512,512]{2,1,0:T(8,128)(2,1)} %w_out.1), custom_call_target="tpu_custom_call" | custom-call | flops 67108864 | bytes 4194304 | tf_op jit(solution)/shard_map/arrange/pallas_call | solution.py:71
  1.8 1.9 %collective-permute-start = (bf16[4,512,512]{2,1,0:T(8,128)(2,1)S(1)}, bf16[4,512,512]{2,1,0:T(8,128)(2,1)S(1)}, u32[]{:S(2)}, u32[]{:S(2)}) collective-permute-start(bf16[4,512,512]{2,1,0:T(8,128)(2,1)S(1)} %get-tuple-element.18.own), channel_id=1, source_target_pairs={{0,256},{256,0},{1,257},{257,1},{2,258},{258,2},{3,259},{259,3},{4... | collective-permute-start | bytes 6291464 | tf_op jit(solution)/shard_map/ppermute | solution.py:383
  3.8 0.0 copy-done
  3.8 2.4 %collective-permute-start.3 = (bf16[1,512,2048]{2,1,0:T(8,128)(2,1)S(1)}, bf16[1,512,2048]{2,1,0:T(8,128)(2,1)S(1)}, u32[]{:S(2)}, u32[]{:S(2)}) collective-permute-start(bf16[1,512,2048]{2,1,0:T(8,128)(2,1)S(1)} %copy-done), channel_id=1, source_target_pairs={{0,256},{256,0},{1,257},{257,1},{2,258},{258,2},{3,259},{259,3},{4... | collective-permute-start | bytes 6291464 | tf_op jit(solution)/shard_map/ppermute | solution.py:386
  6.2 1.9 %collective-permute-start.4 = (bf16[1,2048,512]{2,1,0:T(8,128)(2,1)}, bf16[1,2048,512]{2,1,0:T(8,128)(2,1)S(1)}, u32[]{:S(2)}, u32[]{:S(2)}) collective-permute-start(bf16[1,2048,512]{2,1,0:T(8,128)(2,1)} %down_own.1), channel_id=1, source_target_pairs={{0,256},{256,0},{1,257},{257,1},{2,258},{258,2},{3,259},{259,3},{4... | collective-permute-start | bytes 6291464 | tf_op jit(solution)/shard_map/ppermute | solution.py:387
  8.1 0.0 copy-start.2
  8.1 0.0 copy-start.3
  8.1 6.7 %collective-permute-start.2 = (bf16[256,512]{1,0:T(8,128)(2,1)S(1)}, bf16[256,512]{1,0:T(8,128)(2,1)S(1)}, u32[]{:S(2)}, u32[]{:S(2)}) collective-permute-start(bf16[256,512]{1,0:T(8,128)(2,1)S(1)} %get-tuple-element.17.sent), channel_id=1, source_target_pairs={{1,2},{2,1},{3,4},{4,3},{5,6},{6,5},{7,8},{8,7},{9,10},{10,9},{11,... | collective-permute-start | bytes 786440 | tf_op jit(solution)/shard_map/ppermute | solution.py:381
  14.8 1.9 %collective-permute-start.1 = (bf16[256,512]{1,0:T(8,128)(2,1)S(1)}, bf16[256,512]{1,0:T(8,128)(2,1)S(1)}, u32[]{:S(2)}, u32[]{:S(2)}) collective-permute-start(bf16[256,512]{1,0:T(8,128)(2,1)S(1)} %get-tuple-element.17.sent), channel_id=1, source_target_pairs={{0,1},{1,0},{2,3},{3,2},{4,5},{5,4},{6,7},{7,6},{8,9},{9,8},{10,11... | collective-permute-start | bytes 786440 | tf_op jit(solution)/shard_map/ppermute | solution.py:384
  16.7 0.0 collective-permute-done.came
  16.7 0.7 %shard_map.82 = (bf16[2,4,256,128]{3,2,1,0:T(8,128)(2,1)S(1)}, bf16[256,512]{1,0:T(8,128)(2,1)S(1)}, bf16[2,4,128,128]{3,2,1,0:T(8,128)(2,1)S(1)}) custom-call(bf16[256,512]{1,0:T(8,128)(2,1)S(1)} %get-tuple-element.17.sent, bf16[4,512,512]{2,1,0:T(8,128)(2,1)S(1)} %get-tuple-element.18.own, bf16[4,512,512]{2,1,0:T(8,128)(2,1)S(1)} %collective-permute-done.came), custom_call_target="tpu_custom_call" | custom-call | flops 402653184 | bytes 4194304 | tf_op jit(solution)/shard_map/pallas_call | solution.py:135
  17.4 6.8 %collective-permute-done.2.near_b = bf16[256,512]{1,0:T(8,128)(2,1)S(1)} collective-permute-done((bf16[256,512]{1,0:T(8,128)(2,1)S(1)}, bf16[256,512]{1,0:T(8,128)(2,1)S(1)}, u32[]{:S(2)}, u32[]{:S(2)}) %collective-permute-start.2) | collective-permute-done | bytes 262176 | tf_op jit(solution)/shard_map/ppermute | solution.py:381
  24.2 1.0 %collective-permute-done.1.near_a = bf16[256,512]{1,0:T(8,128)(2,1)S(1)} collective-permute-done((bf16[256,512]{1,0:T(8,128)(2,1)S(1)}, bf16[256,512]{1,0:T(8,128)(2,1)S(1)}, u32[]{:S(2)}, u32[]{:S(2)}) %collective-permute-start.1) | collective-permute-done | bytes 262176 | tf_op jit(solution)/shard_map/ppermute | solution.py:384
  25.1 0.0 copy-done.2
  25.1 0.0 copy-done.3
  25.1 2.3 %shard_map.83.middle = bf16[256,512]{1,0:T(8,128)(2,1)S(1)} custom-call(s32[2,2,3]{2,1,0:T(2,128)S(1)} %copy-done.3, s32[2,256]{1,0:T(2,128)S(1)} %copy-done.2, bf16[256,512]{1,0:T(8,128)(2,1)S(1)} %get-tuple-element.16.state, bf16[2,4,256,128]{3,2,1,0:T(8,128)(2,1)S(1)} %get-tuple-element.19.queries, bf16[256,512]{1,0:T(8,128)(2,1)S(1)} %get-tuple-element.20.own_keys, ...), custom_call_target="tpu_custom_call" | custom-call | flops 1000000000 | bytes 4194304 | tf_op jit(solution)/shard_map/pallas_call | solution.py:268
  27.5 0.0 copy-start.1
  27.5 0.0 collective-permute-done.3.came.up_came
  27.5 1.0 %shard_map.84.hidden = bf16[256,2048]{1,0:T(8,128)(2,1)S(1)} custom-call(bf16[256,512]{1,0:T(8,128)(2,1)S(1)} %shard_map.83.middle, bf16[1,512,2048]{2,1,0:T(8,128)(2,1)S(1)} %copy-done, bf16[1,512,2048]{2,1,0:T(8,128)(2,1)S(1)} %collective-permute-done.3.came.up_came), custom_call_target="tpu_custom_call" | custom-call | flops 536870912 | bytes 3145728 | tf_op jit(solution)/shard_map/pallas_call | solution.py:338
  28.5 0.0 collective-permute-done.4.came.down_came
  28.5 0.5 %copy-done.1 = bf16[1,2048,512]{2,1,0:T(8,128)(2,1)S(1)} copy-done((bf16[1,2048,512]{2,1,0:T(8,128)(2,1)S(1)}, bf16[1,2048,512]{2,1,0:T(8,128)(2,1)}, u32[]{:S(2)}) %copy-start.1) | copy-done | bytes 2097176
  29.1 0.9 %shard_map.85 = (bf16[256,512]{1,0:T(8,128)(2,1)S(1)}, bf16[256,512]{1,0:T(8,128)(2,1)S(1)}) custom-call(bf16[256,2048]{1,0:T(8,128)(2,1)S(1)} %shard_map.84.hidden, bf16[256,512]{1,0:T(8,128)(2,1)S(1)} %shard_map.83.middle, bf16[1,2048,512]{2,1,0:T(8,128)(2,1)S(1)} %copy-done.1, bf16[1,2048,512]{2,1,0:T(8,128)(2,1)S(1)} %collective-permute-done.4.came.down_came), custom_call_target="tpu_custom_call" | custom-call | flops 536870912 | bytes 3145728 | tf_op jit(solution)/shard_map/pallas_call | solution.py:346
  30.0 5.7 %collective-permute-start.6 = (bf16[256,512]{1,0:T(8,128)(2,1)S(1)}, bf16[256,512]{1,0:T(8,128)(2,1)S(1)}, u32[]{:S(2)}, u32[]{:S(2)}) collective-permute-start(bf16[256,512]{1,0:T(8,128)(2,1)S(1)} %get-tuple-element.23.sent), channel_id=1, source_target_pairs={{1,2},{2,1},{3,4},{4,3},{5,6},{6,5},{7,8},{8,7},{9,10},{10,9},{11,... | collective-permute-start | bytes 786440 | tf_op jit(solution)/shard_map/ppermute | solution.py:381
  35.7 1.9 %collective-permute-start.5 = (bf16[256,512]{1,0:T(8,128)(2,1)S(1)}, bf16[256,512]{1,0:T(8,128)(2,1)S(1)}, u32[]{:S(2)}, u32[]{:S(2)}) collective-permute-start(bf16[256,512]{1,0:T(8,128)(2,1)S(1)} %get-tuple-element.23.sent), channel_id=1, source_target_pairs={{0,1},{1,0},{2,3},{3,2},{4,5},{5,4},{6,7},{7,6},{8,9},{9,8},{10,11... | collective-permute-start | bytes 786440 | tf_op jit(solution)/shard_map/ppermute | solution.py:384
  37.6 0.7 %shard_map.86 = (bf16[2,4,256,128]{3,2,1,0:T(8,128)(2,1)S(1)}, bf16[256,512]{1,0:T(8,128)(2,1)S(1)}, bf16[2,4,128,128]{3,2,1,0:T(8,128)(2,1)S(1)}) custom-call(bf16[256,512]{1,0:T(8,128)(2,1)S(1)} %get-tuple-element.23.sent, bf16[4,512,512]{2,1,0:T(8,128)(2,1)S(1)} %get-tuple-element.18.own, bf16[4,512,512]{2,1,0:T(8,128)(2,1)S(1)} %collective-permute-done.came), custom_call_target="tpu_custom_call" | custom-call | flops 402653184 | bytes 4194304 | tf_op jit(solution)/shard_map/pallas_call | solution.py:135
  38.3 6.6 %collective-permute-done.6.near_b = bf16[256,512]{1,0:T(8,128)(2,1)S(1)} collective-permute-done((bf16[256,512]{1,0:T(8,128)(2,1)S(1)}, bf16[256,512]{1,0:T(8,128)(2,1)S(1)}, u32[]{:S(2)}, u32[]{:S(2)}) %collective-permute-start.6) | collective-permute-done | bytes 262176 | tf_op jit(solution)/shard_map/ppermute | solution.py:381
  44.8 0.3 collective-permute-done.5.near_a
  45.1 2.5 %shard_map.87.middle_ref = bf16[256,512]{1,0:T(8,128)(2,1)S(1)} custom-call(s32[2,2,3]{2,1,0:T(2,128)S(1)} %copy-done.3, s32[2,256]{1,0:T(2,128)S(1)} %copy-done.2, bf16[256,512]{1,0:T(8,128)(2,1)S(1)} %get-tuple-element.22.state, bf16[2,4,256,128]{3,2,1,0:T(8,128)(2,1)S(1)} %get-tuple-element.24.queries, bf16[256,512]{1,0:T(8,128)(2,1)S(1)} %get-tuple-element.25.own_keys, ...), custom_call_target="tpu_custom_call" | custom-call | flops 1000000000 | bytes 4194304 | tf_op jit(solution)/shard_map/pallas_call | solution.py:268
  47.6 2.3 %shard_map.88 = bf16[256,512]{1,0:T(8,128)(2,1)} custom-call(s32[2,256]{1,0:T(2,128)S(1)} %copy-done.2, bf16[256,512]{1,0:T(8,128)(2,1)S(1)} %shard_map.87.middle_ref, bf16[1,512,2048]{2,1,0:T(8,128)(2,1)S(1)} %copy-done, bf16[1,2048,512]{2,1,0:T(8,128)(2,1)S(1)} %copy-done.1, bf16[1,512,2048]{2,1,0:T(8,128)(2,1)S(1)} %collective-permute-done.3.came.up_came, ...), custom_call_target="tpu_custom_call" | custom-call | flops 1073741824 | bytes 5242880 | tf_op jit(solution)/shard_map/pallas_call | solution.py:359
Async XLA Ops:
  0.0 3.8 %copy-start = (bf16[1,512,2048]{2,1,0:T(8,128)(2,1)S(1)}, bf16[1,512,2048]{2,1,0:T(8,128)(2,1)}, u32[]{:S(2)}) copy-start(bf16[1,512,2048]{2,1,0:T(8,128)(2,1)} %up_own.1) | copy-start | bytes 6291460
  1.8 14.9 %collective-permute-start = (bf16[4,512,512]{2,1,0:T(8,128)(2,1)S(1)}, bf16[4,512,512]{2,1,0:T(8,128)(2,1)S(1)}, u32[]{:S(2)}, u32[]{:S(2)}) collective-permute-start(bf16[4,512,512]{2,1,0:T(8,128)(2,1)S(1)} %get-tuple-element.18.own), channel_id=1, source_target_pairs={{0,256},{256,0},{1,257},{257,1},{2,258},{258,2},{3,259},{259,3},{4... | collective-permute-start | bytes 6291464 | tf_op jit(solution)/shard_map/ppermute | solution.py:383
  3.8 23.7 %collective-permute-start.3 = (bf16[1,512,2048]{2,1,0:T(8,128)(2,1)S(1)}, bf16[1,512,2048]{2,1,0:T(8,128)(2,1)S(1)}, u32[]{:S(2)}, u32[]{:S(2)}) collective-permute-start(bf16[1,512,2048]{2,1,0:T(8,128)(2,1)S(1)} %copy-done), channel_id=1, source_target_pairs={{0,256},{256,0},{1,257},{257,1},{2,258},{258,2},{3,259},{259,3},{4... | collective-permute-start | bytes 6291464 | tf_op jit(solution)/shard_map/ppermute | solution.py:386
  6.2 22.3 %collective-permute-start.4 = (bf16[1,2048,512]{2,1,0:T(8,128)(2,1)}, bf16[1,2048,512]{2,1,0:T(8,128)(2,1)S(1)}, u32[]{:S(2)}, u32[]{:S(2)}) collective-permute-start(bf16[1,2048,512]{2,1,0:T(8,128)(2,1)} %down_own.1), channel_id=1, source_target_pairs={{0,256},{256,0},{1,257},{257,1},{2,258},{258,2},{3,259},{259,3},{4... | collective-permute-start | bytes 6291464 | tf_op jit(solution)/shard_map/ppermute | solution.py:387
  8.1 17.0 %copy-start.2 = (s32[2,256]{1,0:T(2,128)S(1)}, s32[2,256]{1,0:T(2,128)}, u32[]{:S(2)}) copy-start(s32[2,256]{1,0:T(2,128)} %counts_in.5) | copy-start | bytes 6148
  8.1 17.0 %copy-start.3 = (s32[2,2,3]{2,1,0:T(2,128)S(1)}, s32[2,2,3]{2,1,0:T(2,128)}, u32[]{:S(2)}) copy-start(s32[2,2,3]{2,1,0:T(2,128)} %links_in.3) | copy-start | bytes 148
  8.1 16.0 %collective-permute-start.2 = (bf16[256,512]{1,0:T(8,128)(2,1)S(1)}, bf16[256,512]{1,0:T(8,128)(2,1)S(1)}, u32[]{:S(2)}, u32[]{:S(2)}) collective-permute-start(bf16[256,512]{1,0:T(8,128)(2,1)S(1)} %get-tuple-element.17.sent), channel_id=1, source_target_pairs={{1,2},{2,1},{3,4},{4,3},{5,6},{6,5},{7,8},{8,7},{9,10},{10,9},{11,... | collective-permute-start | bytes 786440 | tf_op jit(solution)/shard_map/ppermute | solution.py:381
  14.8 10.3 %collective-permute-start.1 = (bf16[256,512]{1,0:T(8,128)(2,1)S(1)}, bf16[256,512]{1,0:T(8,128)(2,1)S(1)}, u32[]{:S(2)}, u32[]{:S(2)}) collective-permute-start(bf16[256,512]{1,0:T(8,128)(2,1)S(1)} %get-tuple-element.17.sent), channel_id=1, source_target_pairs={{0,1},{1,0},{2,3},{3,2},{4,5},{5,4},{6,7},{7,6},{8,9},{9,8},{10,11... | collective-permute-start | bytes 786440 | tf_op jit(solution)/shard_map/ppermute | solution.py:384
  27.5 1.6 %copy-start.1 = (bf16[1,2048,512]{2,1,0:T(8,128)(2,1)S(1)}, bf16[1,2048,512]{2,1,0:T(8,128)(2,1)}, u32[]{:S(2)}) copy-start(bf16[1,2048,512]{2,1,0:T(8,128)(2,1)} %down_own.1) | copy-start | bytes 6291460
  30.0 14.9 %collective-permute-start.6 = (bf16[256,512]{1,0:T(8,128)(2,1)S(1)}, bf16[256,512]{1,0:T(8,128)(2,1)S(1)}, u32[]{:S(2)}, u32[]{:S(2)}) collective-permute-start(bf16[256,512]{1,0:T(8,128)(2,1)S(1)} %get-tuple-element.23.sent), channel_id=1, source_target_pairs={{1,2},{2,1},{3,4},{4,3},{5,6},{6,5},{7,8},{8,7},{9,10},{10,9},{11,... | collective-permute-start | bytes 786440 | tf_op jit(solution)/shard_map/ppermute | solution.py:381
  35.7 9.5 %collective-permute-start.5 = (bf16[256,512]{1,0:T(8,128)(2,1)S(1)}, bf16[256,512]{1,0:T(8,128)(2,1)S(1)}, u32[]{:S(2)}, u32[]{:S(2)}) collective-permute-start(bf16[256,512]{1,0:T(8,128)(2,1)S(1)} %get-tuple-element.23.sent), channel_id=1, source_target_pairs={{0,1},{1,0},{2,3},{3,2},{4,5},{5,4},{6,7},{7,6},{8,9},{9,8},{10,11... | collective-permute-start | bytes 786440 | tf_op jit(solution)/shard_map/ppermute | solution.py:384

commit v5 on v4

--- a/solution.py
+++ b/solution.py
@@ -1,4 +1,5 @@
 import functools
+import math
 
 import jax
 import jax.numpy as jnp
@@ -18,6 +19,7 @@
 FF = 2048
 WIDTH = 1024
 LIMIT = 16 << 20
+SCALE = HEAD**-0.5 * math.log2(math.e)
 BF16 = jnp.bfloat16
 F32 = jnp.float32
 
@@ -45,18 +47,18 @@
 
 def arrange_kernel(hits_hbm, order_hbm, w_qkv, w_out, ordered, sent, packed, hits, order, sem):
     event = lax.axis_index("section")
-    pairs = [(hits_hbm.at[0], hits), (order_hbm.at[event], order)]
+    pairs = [(order_hbm.at[event], order), (hits_hbm.at[0], hits)]
     for i in range(3):
         pairs.append((w_qkv.at[0, :, pl.ds(i * D, D)], packed.at[QKV + i]))
     pairs.append((w_out.at[0], packed.at[OUT]))
     copies = copies_of(pairs, sem)
     for copy in copies:
         copy.start()
-    copies[0].wait()
-    copies[1].wait()
     rows = hits.shape[0]
     source_row = lax.broadcasted_iota(jnp.int32, (rows, rows), 0)
+    copies[0].wait()
     chosen = jnp.where(source_row == order[...], 1.0, 0.0).T.astype(BF16)
+    copies[1].wait()
     state = dot(chosen, hits[...]).astype(BF16)
     ordered[...] = state
     sent[...] = normalize(state.astype(F32))
@@ -102,35 +104,54 @@
         body(*came)
 
 
+def match(key, query):
+    return lax.dot_general(key, query, (((1,), (1,)), ((), ())), preferred_element_type=F32)
+
+
 def turned(values, patch, pair):
     part = values[patch * PATCH : (patch + 1) * PATCH, pair * 128 : (pair + 1) * 128]
     return part.T.astype(BF16)
 
 
-def prepare_kernel(block, sent, own, came, queries, keys, values):
+def prepare_kernel(
+    block, counts_in, sent, own, came, queries, keys, values, scores, tops, counts, sem
+):
+    bring = pltpu.make_async_copy(counts_in, counts, sem)
+    bring.start()
     low = lax.broadcasted_iota(jnp.int32, (PATCH, 128), 1) < HEAD
-    scale = jnp.asarray(HEAD**-0.5, BF16)
-    low_scale = jnp.where(low, scale, 0.0).astype(BF16)
-    high_scale = jnp.where(low, 0.0, scale).astype(BF16)
+    key_row = lax.broadcasted_iota(jnp.int32, (PATCH, 2 * PATCH), 0)
+    patches = sent.shape[0] // PATCH
 
     def body(weights):
         normed = sent[...]
-        query = dot(normed, weights[QKV]).astype(BF16)
+        query = dot(normed, weights[QKV]) * SCALE
+        for patch in range(patches):
+            for pair in range(PAIRS):
+                part = query[patch * PATCH : (patch + 1) * PATCH, pair * 128 : (pair + 1) * 128]
+                queries[patch, pair, 0:PATCH, :] = jnp.where(low, part, 0.0).astype(BF16)
+                queries[patch, pair, PATCH : 2 * PATCH, :] = jnp.where(low, 0.0, part).astype(BF16)
         keys[...] = dot(normed, weights[QKV + 1]).astype(BF16)
         value = dot(normed, weights[QKV + 2])
-        for patch in range(sent.shape[0] // PATCH):
-            for pair in range(PAIRS):
-                part = query[patch * PATCH : (patch + 1) * PATCH, pair * 128 : (pair + 1) * 128]
-                queries[patch, pair, 0:PATCH, :] = part * low_scale
-                queries[patch, pair, PATCH : 2 * PATCH, :] = part * high_scale
+        bring.wait()
+        count = counts[lax.axis_index("section"), lax.axis_index("region")]
+        for patch in range(patches):
+            valid = key_row < count - patch * PATCH
+            for pair in range(PAIRS):
+                unit = patch * PAIRS + pair
+                across = slice(pair * 128, (pair + 1) * 128)
+                score = match(keys[patch * PATCH : (patch + 1) * PATCH, across], queries[patch, pair])
+                score = jnp.where(valid, score, -1e30)
+                scores[unit] = score
+                tops[unit] = jnp.broadcast_to(jnp.max(score, axis=0, keepdims=True), (8, 2 * PATCH))
                 values[patch, pair] = turned(value, patch, pair)
 
     with_weights(block, (own,), (came,), body)
 
 
-def prepare(block, sent, own, came):
+def prepare(block, counts, sent, own, came):
     rows = sent.shape[0]
     patches = rows // PATCH
+    units = patches * PAIRS
     vmem = pl.BlockSpec(memory_space=pltpu.VMEM)
     return pl.pallas_call(
         functools.partial(prepare_kernel, block),
@@ -138,14 +159,17 @@
             jax.ShapeDtypeStruct((patches, PAIRS, 2 * PATCH, 128), BF16),
             jax.ShapeDtypeStruct((rows, D), BF16),
             jax.ShapeDtypeStruct((patches, PAIRS, 128, PATCH), BF16),
-        ),
-        in_specs=[vmem] * 3,
-        out_specs=(vmem,) * 3,
+            jax.ShapeDtypeStruct((units, PATCH, 2 * PATCH), F32),
+            jax.ShapeDtypeStruct((units, 8, 2 * PATCH), F32),
+        ),
+        in_specs=[pl.BlockSpec(memory_space=pl.ANY)] + [vmem] * 3,
+        out_specs=(vmem,) * 5,
+        scratch_shapes=[pltpu.SMEM(counts.shape, jnp.int32), pltpu.SemaphoreType.DMA],
         compiler_params=pltpu.CompilerParams(vmem_limit_bytes=LIMIT),
         cost_estimate=pl.CostEstimate(
-            flops=6 * rows * D * D, bytes_accessed=4 << 20, transcendentals=0
-        ),
-    )(sent, own, came)
+            flops=7 * rows * D * D, bytes_accessed=4 << 20, transcendentals=0
+        ),
+    )(counts, sent, own, came)
 
 
 def attend_kernel(
@@ -156,6 +180,8 @@
     queries,
     own_keys,
     own_values,
+    own_scores,
+    own_tops,
     near_a,
     near_b,
     own,
@@ -176,15 +202,7 @@
     regions = counts.shape[1]
     rows = state.shape[0]
     patches = rows // PATCH
-    bring = copies_of(
-        [
-            (links_in, links),
-            (counts_in, counts),
-            (own_keys, keys.at[pl.ds(0, rows)]),
-            (own_values, values.at[pl.ds(0, patches)]),
-        ],
-        sem,
-    )
+    bring = copies_of([(links_in, links), (counts_in, counts)], sem)
     for copy in bring:
         copy.start()
     even = lax.rem(region, 2) == 0
@@ -200,6 +218,8 @@
             for pair in range(PAIRS):
                 values[patches + patch, pair] = turned(value, patch, pair)
         keys[rows : 3 * rows, :] = dot(normed, weights[QKV + 1]).astype(BF16)
+        keys[0:rows, :] = own_keys[...]
+        values[0:patches] = own_values[...]
         for copy in bring:
             copy.wait()
         count_own = counts[event, region]
@@ -208,10 +228,10 @@
         slots = []
         for patch in range(patches):
             valid = []
-            for link in range(LINKS):
+            for link in range(1, LINKS):
                 linked = links[event, patch, link]
-                owner = lax.div(linked, patches)
-                half = lax.rem(linked, patches)
+                owner = jnp.right_shift(linked, 1)
+                half = jnp.bitwise_and(linked, 1)
                 base = jnp.where(owner == region, 0, jnp.where(owner == region_a, 1, 2))
                 count = jnp.where(base == 0, count_own, jnp.where(base == 1, count_a, count_b))
                 slots.append(base * patches + half)
@@ -220,24 +240,29 @@
                 unit = patch * PAIRS + pair
                 query = queries[patch, pair]
                 top = None
-                for link in range(LINKS):
-                    start = pl.multiple_of(slots[patch * LINKS + link] * PATCH, PATCH)
-                    score = lax.dot_general(
-                        keys[pl.ds(start, PATCH), pair * 128 : (pair + 1) * 128],
-                        query,
-                        (((1,), (1,)), ((), ())),
-                        preferred_element_type=F32,
-                    )
-                    score = jnp.where(valid[link], score, -1e30)
-                    scores[unit, link * PATCH : (link + 1) * PATCH, :] = score
+                for link in range(1, LINKS):
+                    start = pl.multiple_of(slots[patch * (LINKS - 1) + link - 1] * PATCH, PATCH)
+                    key = keys[pl.ds(start, PATCH), pair * 128 : (pair + 1) * 128]
+                    score = jnp.where(valid[link - 1], match(key, query), -1e30)
+                    scores[unit, (link - 1) * PATCH : link * PATCH, :] = score
                     top = score if top is None else jnp.maximum(top, score)
-                tops[unit] = jnp.broadcast_to(jnp.max(top, axis=0, keepdims=True), (8, 2 * PATCH))
+                top = jnp.broadcast_to(jnp.max(top, axis=0, keepdims=True), (8, 2 * PATCH))
+                tops[unit] = jnp.maximum(top, own_tops[unit])
         for patch in range(patches):
             for pair in range(PAIRS):
                 unit = patch * PAIRS + pair
-                weighed = jnp.exp(scores[unit] - tops[unit, 0:1, :]).astype(BF16)
+                top = tops[unit, 0:1, :]
+                near_slots = slots[patch * (LINKS - 1) : (patch + 1) * (LINKS - 1)]
+                weighed = jnp.concatenate(
+                    [
+                        jnp.exp2(own_scores[unit] - top).astype(BF16),
+                        jnp.exp2(scores[unit] - top).astype(BF16),
+                    ],
+                    axis=0,
+                )
                 taken = jnp.concatenate(
-                    [values[slot, pair] for slot in slots[patch * LINKS : (patch + 1) * LINKS]],
+                    [own_values[patch, pair]]
+                    + [values[slot, pair] for slot in near_slots],
                     axis=1,
                 )
                 totals[unit] = dot(jnp.concatenate([taken, ones], axis=0), weighed)
@@ -260,7 +285,7 @@
     with_weights(block, (own,), (came,), body)
 
 
-def attend(block, links, counts, state, queries, keys, values, near_a, near_b, own, came):
+def attend(block, links, counts, state, prepared, near_a, near_b, own, came):
     rows = state.shape[0]
     patches = rows // PATCH
     vmem = pl.BlockSpec(memory_space=pltpu.VMEM)
@@ -268,24 +293,24 @@
     return pl.pallas_call(
         functools.partial(attend_kernel, block),
         out_shape=jax.ShapeDtypeStruct((rows, D), BF16),
-        in_specs=[any_space] * 2 + [vmem] * 2 + [any_space] * 2 + [vmem] * 4,
+        in_specs=[any_space] * 2 + [vmem] * 10,
         out_specs=vmem,
         scratch_shapes=[
             pltpu.VMEM((3 * rows, D), BF16),
             pltpu.VMEM((3 * patches, PAIRS, 128, PATCH), BF16),
-            pltpu.VMEM((patches * PAIRS, LINKS * PATCH, 2 * PATCH), F32),
+            pltpu.VMEM((patches * PAIRS, (LINKS - 1) * PATCH, 2 * PATCH), F32),
             pltpu.VMEM((patches * PAIRS, 8, 2 * PATCH), F32),
             pltpu.VMEM((patches * PAIRS, 144, 2 * PATCH), F32),
             pltpu.VMEM((rows, D), BF16),
             pltpu.SMEM(links.shape, jnp.int32),
             pltpu.SMEM(counts.shape, jnp.int32),
-            pltpu.SemaphoreType.DMA((4,)),
+            pltpu.SemaphoreType.DMA((2,)),
         ],
         compiler_params=pltpu.CompilerParams(vmem_limit_bytes=LIMIT),
         cost_estimate=pl.CostEstimate(
             flops=10**9, bytes_accessed=4 << 20, transcendentals=8 * 10**5
         ),
-    )(links, counts, state, queries, keys, values, near_a, near_b, own, came)
+    )(links, counts, state, *prepared, near_a, near_b, own, came)
 
 
 def raise_kernel(block, middle, own, came, hidden):
@@ -386,20 +411,8 @@
             up_came = lax.ppermute(w_up, "section", swap)
             down_came = lax.ppermute(w_down, "section", swap)
             second = (w_up, w_down, up_came, down_came)
-        queries, keys, values = prepare(block, sent, own, came)
-        middle = attend(
-            block,
-            links,
-            counts,
-            state,
-            queries,
-            keys,
-            values,
-            near_a,
-            near_b,
-            own,
-            came,
-        )
+        prepared = prepare(block, counts, sent, own, came)
+        middle = attend(block, links, counts, state, prepared, near_a, near_b, own, came)
         if block == 0:
             state, sent = feed_parts(block, middle, *second)
         else:

time: 50.4 us -> 49.7 us (0.986)
  waiting for transfers between devices: 14.6 us -> 14 us
    pallas_call x2, Pallas kernels: 4.82 us -> 4.16 us  [attend(): pl.pallas_call(functools.partial(attend_kernel, block), out_shape=jax.Sha...]
    pallas_call x2, Pallas kernels: 1.33 us -> 1.92 us  [prepare(): pl.pallas_call(functools.partial(prepare_kernel, block), out_shape=(jax.S...]
    ppermute x2, waiting for transfers between devices: 13.3 us -> 12.7 us  [per_device(): near_b = lax.ppermute(sent, 'region', pairs_b)]
  transfers between devices with their start and end apart: 7 -> 7, of which waited for: 4 -> 4; matrix products, arithmetic and copies ran while one was open for 0% -> 0% of each run, Pallas kernels for 9% -> 10%
where the time goes in v5:
time: 49.7 us; the launch traced here: 49.4 us
  starting transfers between devices  22.5 us (45%)
  waiting for transfers between devices  14 us (28%)
  Pallas kernels  12.1 us (24%)
  local copies, waits for them, and re-layouts  0.57 us (1%)
    ppermute x2, waiting for transfers between devices, per_device(): near_b = lax.ppermute(sent, 'region', pairs_b)  12.7 us
    ppermute x2, starting transfers between devices, per_device(): near_b = lax.ppermute(sent, 'region', pairs_b)  12.4 us
    pallas_call x2, Pallas kernels, attend(): pl.pallas_call(functools.partial(attend_kernel, block), out_shape=jax.Sha...  4.16 us
    ppermute x2, starting transfers between devices, per_device(): near_a = lax.ppermute(sent, 'region', pairs_a)  3.84 us
    ppermute x1, starting transfers between devices, per_device(): up_came = lax.ppermute(w_up, 'section', swap)  2.41 us
    pallas_call x1, Pallas kernels, feed(): pl.pallas_call(functools.partial(feed_kernel, block), out_shape=jax.Shape...  2.26 us
    ppermute x1, starting transfers between devices, per_device(): down_came = lax.ppermute(w_down, 'section', swap)  1.92 us
    ppermute x1, starting transfers between devices, per_device(): came = lax.ppermute(own, 'section', swap)  1.92 us
  transfers between devices with their start and end apart: 7, of which 4 were waited for; matrix products, arithmetic and copies ran while one was open for 0% of the time, Pallas kernels for 10%

profile of v5, /device:TPU:256, one launch (start us, length us, event | category | flops | bytes accessed | tf_op | source)
XLA Modules:
  0.0 49.4 jit_solution(17261469970375781453)
XLA Ops:
  0.0 0.0 copy-start
  0.0 0.0 copy-start.2
  0.0 1.8 %arrange.1 = (bf16[256,512]{1,0:T(8,128)(2,1)S(1)}, bf16[256,512]{1,0:T(8,128)(2,1)S(1)}, bf16[4,512,512]{2,1,0:T(8,128)(2,1)S(1)}) custom-call(bf16[1,256,512]{2,1,0:T(8,128)(2,1)} %hits_hbm.1, s32[2,1,256]{2,1,0:T(1,128)} %order_hbm.1, bf16[1,512,1536]{2,1,0:T(8,128)(2,1)} %w_qkv.1, bf16[1,512,512]{2,1,0:T(8,128)(2,1)} %w_out.1), custom_call_target="tpu_custom_call" | custom-call | flops 67108864 | bytes 4194304 | tf_op jit(solution)/shard_map/arrange/pallas_call | solution.py:73
  1.8 1.9 %collective-permute-start = (bf16[4,512,512]{2,1,0:T(8,128)(2,1)S(1)}, bf16[4,512,512]{2,1,0:T(8,128)(2,1)S(1)}, u32[]{:S(2)}, u32[]{:S(2)}) collective-permute-start(bf16[4,512,512]{2,1,0:T(8,128)(2,1)S(1)} %get-tuple-element.22.own), channel_id=1, source_target_pairs={{0,256},{256,0},{1,257},{257,1},{2,258},{258,2},{3,259},{259,3},{4... | collective-permute-start | bytes 6291464 | tf_op jit(solution)/shard_map/ppermute | solution.py:408
  3.8 0.0 copy-done
  3.8 2.4 %collective-permute-start.3 = (bf16[1,512,2048]{2,1,0:T(8,128)(2,1)S(1)}, bf16[1,512,2048]{2,1,0:T(8,128)(2,1)S(1)}, u32[]{:S(2)}, u32[]{:S(2)}) collective-permute-start(bf16[1,512,2048]{2,1,0:T(8,128)(2,1)S(1)} %copy-done), channel_id=1, source_target_pairs={{0,256},{256,0},{1,257},{257,1},{2,258},{258,2},{3,259},{259,3},{4... | collective-permute-start | bytes 6291464 | tf_op jit(solution)/shard_map/ppermute | solution.py:411
  6.2 1.9 %collective-permute-start.4 = (bf16[1,2048,512]{2,1,0:T(8,128)(2,1)}, bf16[1,2048,512]{2,1,0:T(8,128)(2,1)S(1)}, u32[]{:S(2)}, u32[]{:S(2)}) collective-permute-start(bf16[1,2048,512]{2,1,0:T(8,128)(2,1)} %down_own.1), channel_id=1, source_target_pairs={{0,256},{256,0},{1,257},{257,1},{2,258},{258,2},{3,259},{259,3},{4... | collective-permute-start | bytes 6291464 | tf_op jit(solution)/shard_map/ppermute | solution.py:412
  8.1 0.0 copy-start.3
  8.1 6.7 %collective-permute-start.2 = (bf16[256,512]{1,0:T(8,128)(2,1)S(1)}, bf16[256,512]{1,0:T(8,128)(2,1)S(1)}, u32[]{:S(2)}, u32[]{:S(2)}) collective-permute-start(bf16[256,512]{1,0:T(8,128)(2,1)S(1)} %get-tuple-element.21.sent), channel_id=1, source_target_pairs={{1,2},{2,1},{3,4},{4,3},{5,6},{6,5},{7,8},{8,7},{9,10},{10,9},{11,... | collective-permute-start | bytes 786440 | tf_op jit(solution)/shard_map/ppermute | solution.py:406
  14.8 1.9 %collective-permute-start.1 = (bf16[256,512]{1,0:T(8,128)(2,1)S(1)}, bf16[256,512]{1,0:T(8,128)(2,1)S(1)}, u32[]{:S(2)}, u32[]{:S(2)}) collective-permute-start(bf16[256,512]{1,0:T(8,128)(2,1)S(1)} %get-tuple-element.21.sent), channel_id=1, source_target_pairs={{0,1},{1,0},{2,3},{3,2},{4,5},{5,4},{6,7},{7,6},{8,9},{9,8},{10,11... | collective-permute-start | bytes 786440 | tf_op jit(solution)/shard_map/ppermute | solution.py:409
  16.7 0.0 collective-permute-done.came
  16.7 0.0 copy-done.2
  16.8 0.9 %shard_map.82 = (bf16[2,4,256,128]{3,2,1,0:T(8,128)(2,1)S(1)}, bf16[256,512]{1,0:T(8,128)(2,1)S(1)}, bf16[2,4,128,128]{3,2,1,0:T(8,128)(2,1)S(1)}, f32[8,128,256]{2,1,0:T(8,128)S(1)}, f32[8,8,256]{2,1,0:T(8,128)S(1)}) custom-call(s32[2,256]{1,0:T(2,128)S(1)} %copy-done.2, bf16[256,512]{1,0:T(8,128)(2,1)S(1)} %get-tuple-element.21.sent, ...), custom_call_target="tpu_custom_call" | custom-call | flops 469762048 | bytes 4194304 | tf_op jit(solution)/shard_map/pallas_call | solution.py:156
  17.7 6.5 %collective-permute-done.2.near_b = bf16[256,512]{1,0:T(8,128)(2,1)S(1)} collective-permute-done((bf16[256,512]{1,0:T(8,128)(2,1)S(1)}, bf16[256,512]{1,0:T(8,128)(2,1)S(1)}, u32[]{:S(2)}, u32[]{:S(2)}) %collective-permute-start.2) | collective-permute-done | bytes 262176 | tf_op jit(solution)/shard_map/ppermute | solution.py:406
  24.2 1.0 %collective-permute-done.1.near_a = bf16[256,512]{1,0:T(8,128)(2,1)S(1)} collective-permute-done((bf16[256,512]{1,0:T(8,128)(2,1)S(1)}, bf16[256,512]{1,0:T(8,128)(2,1)S(1)}, u32[]{:S(2)}, u32[]{:S(2)}) %collective-permute-start.1) | collective-permute-done | bytes 262176 | tf_op jit(solution)/shard_map/ppermute | solution.py:409
  25.1 0.0 copy-done.3
  25.1 2.1 %shard_map.83.middle = bf16[256,512]{1,0:T(8,128)(2,1)S(1)} custom-call(s32[2,2,3]{2,1,0:T(2,128)S(1)} %copy-done.3, s32[2,256]{1,0:T(2,128)S(1)} %copy-done.2, bf16[256,512]{1,0:T(8,128)(2,1)S(1)} %get-tuple-element.20.state, bf16[2,4,256,128]{3,2,1,0:T(8,128)(2,1)S(1)} %get-tuple-element.23.queries, bf16[256,512]{1,0:T(8,128)(2,1)S(1)} %get-tuple-element.24.own_keys, ...), custom_call_target="tpu_custom_call" | custom-call | flops 1000000000 | bytes 4194304 | tf_op jit(solution)/shard_map/pallas_call | solution.py:293
  27.2 0.0 copy-start.1
  27.2 0.0 collective-permute-done.3.came.up_came
  27.2 1.0 %shard_map.84.hidden = bf16[256,2048]{1,0:T(8,128)(2,1)S(1)} custom-call(bf16[256,512]{1,0:T(8,128)(2,1)S(1)} %shard_map.83.middle, bf16[1,512,2048]{2,1,0:T(8,128)(2,1)S(1)} %copy-done, bf16[1,512,2048]{2,1,0:T(8,128)(2,1)S(1)} %collective-permute-done.3.came.up_came), custom_call_target="tpu_custom_call" | custom-call | flops 536870912 | bytes 3145728 | tf_op jit(solution)/shard_map/pallas_call | solution.py:363
  28.3 0.0 collective-permute-done.4.came.down_came
  28.3 0.6 %copy-done.1 = bf16[1,2048,512]{2,1,0:T(8,128)(2,1)S(1)} copy-done((bf16[1,2048,512]{2,1,0:T(8,128)(2,1)S(1)}, bf16[1,2048,512]{2,1,0:T(8,128)(2,1)}, u32[]{:S(2)}) %copy-start.1) | copy-done | bytes 2097176
  28.8 0.9 %shard_map.85 = (bf16[256,512]{1,0:T(8,128)(2,1)S(1)}, bf16[256,512]{1,0:T(8,128)(2,1)S(1)}) custom-call(bf16[256,2048]{1,0:T(8,128)(2,1)S(1)} %shard_map.84.hidden, bf16[256,512]{1,0:T(8,128)(2,1)S(1)} %shard_map.83.middle, bf16[1,2048,512]{2,1,0:T(8,128)(2,1)S(1)} %copy-done.1, bf16[1,2048,512]{2,1,0:T(8,128)(2,1)S(1)} %collective-permute-done.4.came.down_came), custom_call_target="tpu_custom_call" | custom-call | flops 536870912 | bytes 3145728 | tf_op jit(solution)/shard_map/pallas_call | solution.py:371
  29.7 5.7 %collective-permute-start.6 = (bf16[256,512]{1,0:T(8,128)(2,1)S(1)}, bf16[256,512]{1,0:T(8,128)(2,1)S(1)}, u32[]{:S(2)}, u32[]{:S(2)}) collective-permute-start(bf16[256,512]{1,0:T(8,128)(2,1)S(1)} %get-tuple-element.29.sent), channel_id=1, source_target_pairs={{1,2},{2,1},{3,4},{4,3},{5,6},{6,5},{7,8},{8,7},{9,10},{10,9},{11,... | collective-permute-start | bytes 786440 | tf_op jit(solution)/shard_map/ppermute | solution.py:406
  35.4 1.9 %collective-permute-start.5 = (bf16[256,512]{1,0:T(8,128)(2,1)S(1)}, bf16[256,512]{1,0:T(8,128)(2,1)S(1)}, u32[]{:S(2)}, u32[]{:S(2)}) collective-permute-start(bf16[256,512]{1,0:T(8,128)(2,1)S(1)} %get-tuple-element.29.sent), channel_id=1, source_target_pairs={{0,1},{1,0},{2,3},{3,2},{4,5},{5,4},{6,7},{7,6},{8,9},{9,8},{10,11... | collective-permute-start | bytes 786440 | tf_op jit(solution)/shard_map/ppermute | solution.py:409
  37.4 1.0 %shard_map.86 = (bf16[2,4,256,128]{3,2,1,0:T(8,128)(2,1)S(1)}, bf16[256,512]{1,0:T(8,128)(2,1)S(1)}, bf16[2,4,128,128]{3,2,1,0:T(8,128)(2,1)S(1)}, f32[8,128,256]{2,1,0:T(8,128)S(1)}, f32[8,8,256]{2,1,0:T(8,128)S(1)}) custom-call(s32[2,256]{1,0:T(2,128)S(1)} %copy-done.2, bf16[256,512]{1,0:T(8,128)(2,1)S(1)} %get-tuple-element.29.sent, ...), custom_call_target="tpu_custom_call" | custom-call | flops 469762048 | bytes 4194304 | tf_op jit(solution)/shard_map/pallas_call | solution.py:156
  38.4 6.2 %collective-permute-done.6.near_b = bf16[256,512]{1,0:T(8,128)(2,1)S(1)} collective-permute-done((bf16[256,512]{1,0:T(8,128)(2,1)S(1)}, bf16[256,512]{1,0:T(8,128)(2,1)S(1)}, u32[]{:S(2)}, u32[]{:S(2)}) %collective-permute-start.6) | collective-permute-done | bytes 262176 | tf_op jit(solution)/shard_map/ppermute | solution.py:406
  44.6 0.3 collective-permute-done.5.near_a
  44.9 2.1 %shard_map.87.middle_ref = bf16[256,512]{1,0:T(8,128)(2,1)S(1)} custom-call(s32[2,2,3]{2,1,0:T(2,128)S(1)} %copy-done.3, s32[2,256]{1,0:T(2,128)S(1)} %copy-done.2, bf16[256,512]{1,0:T(8,128)(2,1)S(1)} %get-tuple-element.28.state, bf16[2,4,256,128]{3,2,1,0:T(8,128)(2,1)S(1)} %get-tuple-element.30.queries, bf16[256,512]{1,0:T(8,128)(2,1)S(1)} %get-tuple-element.31.own_keys, ...), custom_call_target="tpu_custom_call" | custom-call | flops 1000000000 | bytes 4194304 | tf_op jit(solution)/shard_map/pallas_call | solution.py:293
  47.0 2.3 %shard_map.88 = bf16[256,512]{1,0:T(8,128)(2,1)} custom-call(s32[2,256]{1,0:T(2,128)S(1)} %copy-done.2, bf16[256,512]{1,0:T(8,128)(2,1)S(1)} %shard_map.87.middle_ref, bf16[1,512,2048]{2,1,0:T(8,128)(2,1)S(1)} %copy-done, bf16[1,2048,512]{2,1,0:T(8,128)(2,1)S(1)} %copy-done.1, bf16[1,512,2048]{2,1,0:T(8,128)(2,1)S(1)} %collective-permute-done.3.came.up_came, ...), custom_call_target="tpu_custom_call" | custom-call | flops 1073741824 | bytes 5242880 | tf_op jit(solution)/shard_map/pallas_call | solution.py:384
Async XLA Ops:
  0.0 3.8 %copy-start = (bf16[1,512,2048]{2,1,0:T(8,128)(2,1)S(1)}, bf16[1,512,2048]{2,1,0:T(8,128)(2,1)}, u32[]{:S(2)}) copy-start(bf16[1,512,2048]{2,1,0:T(8,128)(2,1)} %up_own.1) | copy-start | bytes 6291460
  0.0 16.7 %copy-start.2 = (s32[2,256]{1,0:T(2,128)S(1)}, s32[2,256]{1,0:T(2,128)}, u32[]{:S(2)}) copy-start(s32[2,256]{1,0:T(2,128)} %counts_in.9) | copy-start | bytes 6148
  1.8 14.9 %collective-permute-start = (bf16[4,512,512]{2,1,0:T(8,128)(2,1)S(1)}, bf16[4,512,512]{2,1,0:T(8,128)(2,1)S(1)}, u32[]{:S(2)}, u32[]{:S(2)}) collective-permute-start(bf16[4,512,512]{2,1,0:T(8,128)(2,1)S(1)} %get-tuple-element.22.own), channel_id=1, source_target_pairs={{0,256},{256,0},{1,257},{257,1},{2,258},{258,2},{3,259},{259,3},{4... | collective-permute-start | bytes 6291464 | tf_op jit(solution)/shard_map/ppermute | solution.py:408
  3.8 23.5 %collective-permute-start.3 = (bf16[1,512,2048]{2,1,0:T(8,128)(2,1)S(1)}, bf16[1,512,2048]{2,1,0:T(8,128)(2,1)S(1)}, u32[]{:S(2)}, u32[]{:S(2)}) collective-permute-start(bf16[1,512,2048]{2,1,0:T(8,128)(2,1)S(1)} %copy-done), channel_id=1, source_target_pairs={{0,256},{256,0},{1,257},{257,1},{2,258},{258,2},{3,259},{259,3},{4... | collective-permute-start | bytes 6291464 | tf_op jit(solution)/shard_map/ppermute | solution.py:411
  6.2 22.1 %collective-permute-start.4 = (bf16[1,2048,512]{2,1,0:T(8,128)(2,1)}, bf16[1,2048,512]{2,1,0:T(8,128)(2,1)S(1)}, u32[]{:S(2)}, u32[]{:S(2)}) collective-permute-start(bf16[1,2048,512]{2,1,0:T(8,128)(2,1)} %down_own.1), channel_id=1, source_target_pairs={{0,256},{256,0},{1,257},{257,1},{2,258},{258,2},{3,259},{259,3},{4... | collective-permute-start | bytes 6291464 | tf_op jit(solution)/shard_map/ppermute | solution.py:412
  8.1 17.0 %copy-start.3 = (s32[2,2,3]{2,1,0:T(2,128)S(1)}, s32[2,2,3]{2,1,0:T(2,128)}, u32[]{:S(2)}) copy-start(s32[2,2,3]{2,1,0:T(2,128)} %links_in.3) | copy-start | bytes 148
  8.1 16.0 %collective-permute-start.2 = (bf16[256,512]{1,0:T(8,128)(2,1)S(1)}, bf16[256,512]{1,0:T(8,128)(2,1)S(1)}, u32[]{:S(2)}, u32[]{:S(2)}) collective-permute-start(bf16[256,512]{1,0:T(8,128)(2,1)S(1)} %get-tuple-element.21.sent), channel_id=1, source_target_pairs={{1,2},{2,1},{3,4},{4,3},{5,6},{6,5},{7,8},{8,7},{9,10},{10,9},{11,... | collective-permute-start | bytes 786440 | tf_op jit(solution)/shard_map/ppermute | solution.py:406
  14.8 10.3 %collective-permute-start.1 = (bf16[256,512]{1,0:T(8,128)(2,1)S(1)}, bf16[256,512]{1,0:T(8,128)(2,1)S(1)}, u32[]{:S(2)}, u32[]{:S(2)}) collective-permute-start(bf16[256,512]{1,0:T(8,128)(2,1)S(1)} %get-tuple-element.21.sent), channel_id=1, source_target_pairs={{0,1},{1,0},{2,3},{3,2},{4,5},{5,4},{6,7},{7,6},{8,9},{9,8},{10,11... | collective-permute-start | bytes 786440 | tf_op jit(solution)/shard_map/ppermute | solution.py:409
  27.2 1.6 %copy-start.1 = (bf16[1,2048,512]{2,1,0:T(8,128)(2,1)S(1)}, bf16[1,2048,512]{2,1,0:T(8,128)(2,1)}, u32[]{:S(2)}) copy-start(bf16[1,2048,512]{2,1,0:T(8,128)(2,1)} %down_own.1) | copy-start | bytes 6291460
  29.7 14.9 %collective-permute-start.6 = (bf16[256,512]{1,0:T(8,128)(2,1)S(1)}, bf16[256,512]{1,0:T(8,128)(2,1)S(1)}, u32[]{:S(2)}, u32[]{:S(2)}) collective-permute-start(bf16[256,512]{1,0:T(8,128)(2,1)S(1)} %get-tuple-element.29.sent), channel_id=1, source_target_pairs={{1,2},{2,1},{3,4},{4,3},{5,6},{6,5},{7,8},{8,7},{9,10},{10,9},{11,... | collective-permute-start | bytes 786440 | tf_op jit(solution)/shard_map/ppermute | solution.py:406
  35.4 9.5 %collective-permute-start.5 = (bf16[256,512]{1,0:T(8,128)(2,1)S(1)}, bf16[256,512]{1,0:T(8,128)(2,1)S(1)}, u32[]{:S(2)}, u32[]{:S(2)}) collective-permute-start(bf16[256,512]{1,0:T(8,128)(2,1)S(1)} %get-tuple-element.29.sent), channel_id=1, source_target_pairs={{0,1},{1,0},{2,3},{3,2},{4,5},{5,4},{6,7},{7,6},{8,9},{9,8},{10,11... | collective-permute-start | bytes 786440 | tf_op jit(solution)/shard_map/ppermute | solution.py:409
